TPU v7x, 256 devices: a whole 4x4x8 slice. The times are simulated.
256 devices in a mesh: feat: 16 (over z, y_lo), cand: 16 (over x, y_hi, core).
Axes of the slice: x: 4, y: 4 (y_hi: 2, y_lo: 2; y = y_hi * 2 + y_lo), z: 8, core: 2. Of those that a mesh axis runs over, the one named last changes fastest.
Arguments:
- cand_grads: bfloat16 [1024, 1048576], P('cand', 'feat'), may hold values from -30 to 30
- val_grads: bfloat16 [256, 1048576], P('cand', 'feat'), may hold values from -30 to 30
- second_moment: float32 [1048576], P('feat'), may hold values from 0.0005 to 1.5
- slot_blocks: int32 [8, 128], replicated, may hold values from 0 to 127, as said below
- slot_seeds: int32 [8, 128], replicated, may hold values from 0 to 1073741823
Outputs:
- scores: float32 [1024, 64], P('cand', 'feat')
Inputs may be any that keep to these rules, and one draw needn't show every extreme that they name: `slot_blocks`: each row is a permutation of the input blocks; with L = 128 / (devices of feat), G = (devices of feat) / 8, and o_k = k * G for even k and (k - 1) * G + 1 for odd k, slot k of output block b reads an input block whose index divided by L equals (b / L + o_k) modulo the devices of feat (divisions rounded down).
All inputs are finite; a program needn't handle non-finite values.
Results may differ from a plain program's by a relative error of at most 0.0003.
Values sent between devices are 32-bit elements; how exact they have to be, the bound alone decides.
No kernel may reach another device: no remote copies, remote signals or barrier semaphores. Data moves between devices by JAX's collectives and lax.ppermute only.
A program may use at most 64 MiB of HBM per device.

v0:
```python
import math

import jax
import jax.numpy as jnp
from jax import lax
from jax.sharding import PartitionSpec as P

PB = 8192
FEATS = 8192
FB = 64
SLOTS = 8
VPT = 4


def block_signs(seed_val, height, breadth):
    across = lax.broadcasted_iota(jnp.int32, (height, breadth), 0)
    column = lax.broadcasted_iota(jnp.int32, (height, breadth), 1)
    mixed = seed_val ^ across * jnp.int32(73856093) ^ column * jnp.int32(19349663)
    for repeat in range(2):
        mixed = mixed ^ lax.shift_right_logical(mixed, jnp.int32(16))
        mixed = mixed * jnp.int32(73244475)
    mixed = mixed ^ lax.shift_right_logical(mixed, jnp.int32(16))
    return (2 * (mixed & 1) - 1).astype(jnp.float32)


def signs_for(seed_val):
    return block_signs(seed_val, PB, FB)


def squares(features):
    return jnp.sum(features * features, axis=(0, 2))


def body(cand_grads, val_grads, second_moment, slot_blocks, slot_seeds):
    local_blocks = second_moment.shape[0] // PB
    first_block = lax.axis_index("feat") * local_blocks
    groups = FEATS // 128
    per_group = 128 // FB
    factor = 1.0 / math.sqrt(SLOTS * PB)
    ncand = cand_grads.shape[0]
    wide = cand_grads.astype(jnp.float32)
    adam_grads = (
        wide / (jnp.sqrt(0.999 * second_moment[None, :] + 0.001 * wide * wide) + 1e-08)
    ).astype(jnp.bfloat16)
    rows_all = jnp.concatenate([adam_grads, val_grads], axis=0)
    height = rows_all.shape[0]

    def one_block(position, summed):
        segment = lax.dynamic_slice_in_dim(rows_all, position * PB, PB, 1)
        matches = (slot_blocks == first_block + position).astype(jnp.int32)
        seeds_now = jnp.sum(slot_seeds * matches, axis=1)
        matrices = (jax.vmap(signs_for)(seeds_now) * factor).astype(jnp.bfloat16)
        partial_out = jnp.einsum(
            "rp,kpf->rkf", segment, matrices, preferred_element_type=jnp.float32
        )
        placing = matches.astype(jnp.float32).reshape(SLOTS, groups, per_group)
        return summed + jnp.einsum(
            "rkf,kgh->grhf", partial_out, placing, precision=lax.Precision.HIGHEST
        )

    start_sum = jnp.zeros((groups, height, per_group, FB), jnp.float32)
    summed = lax.fori_loop(0, local_blocks, one_block, start_sum)
    mine = lax.psum_scatter(
        summed.reshape(groups, height, 128), "feat", scatter_dimension=0, tiled=True
    )
    cand_part = mine[:, :ncand, :]
    val_part = mine[:, ncand:, :]
    cand_sq, val_sq = lax.psum((squares(cand_part), squares(val_part)), "feat")
    val_unit = val_part / jnp.sqrt(val_sq + 1e-06)[None, :, None]
    val_all = lax.all_gather(val_unit, "cand", axis=1, tiled=True)
    dots = jnp.einsum("gih,gvh->iv", cand_part, val_all, precision=lax.Precision.HIGHEST)
    tile = jnp.sum(dots.reshape(ncand, -1, VPT), axis=2) / VPT
    total = lax.psum(tile, "feat")
    width_own = total.shape[1] // lax.axis_size("feat")
    owned = lax.dynamic_slice_in_dim(total, lax.axis_index("feat") * width_own, width_own, 1)
    cand_norm = jnp.sqrt(cand_sq + 1e-06)
    return owned / cand_norm[:, None]


def solution(mesh):
    placed = (P("cand", "feat"), P("cand", "feat"), P("feat"), P(), P())
    return jax.shard_map(
        body, mesh=mesh, in_specs=placed, out_specs=P("cand", "feat"), check_vma=False
    )
```

profile of v0, /device:TPU:0, one launch (start us, length us, event | category | flops | bytes accessed | tf_op | source)
XLA Modules:
  0.0 388.0 jit_solution(3409171600617798099)
XLA Ops:
  6.5 0.0 copy-start
  6.5 0.0 reduce-scatter.2.cloned.1.call-start
  6.5 1.1 broadcast_multiply_fusion
  7.7 0.8 copy.16
  8.5 0.8 copy.17
  9.2 9.5 %fusion.14 = bf16[64,65536]{1,0:T(8,128)(2,1)S(1)} fusion(bf16[64,65536]{1,0:T(8,128)(2,1)} %param.7, f32[65536]{0:T(1024)S(1)} %broadcast_multiply_fusion), kind=kLoop, calls=%fused_computation.25 | loop fusion | flops 29360128 | bytes 17039360 | tf_op jit(solution)/shard_map/convert_element_type | solution.py:44
  18.8 0.0 copy-done
  18.8 6.3 %pad_maximum_fusion = bf16[80,65536]{1,0:T(8,128)(2,1)} fusion(bf16[16,65536]{1,0:T(8,128)(2,1)S(1)} %copy-done, bf16[64,65536]{1,0:T(8,128)(2,1)S(1)} %fusion.14), kind=kLoop, calls=%fused_computation.29 | loop fusion | flops 20971520 | bytes 20971520 | tf_op jit(solution)/shard_map/concatenate | solution.py:45
  25.1 148.3 %while.16 = (s32[]{:T(128)}, f32[64,80,2,64]{1,0,3,2:T(8,128)}, s32[]{:T(128)}, s32[8,128]{0,1:T(8,128)S(1)}, bf16[80,65536]{1,0:T(8,128)(2,1)}, /*index=5*/s32[...) while((s32[]{:T(128)}, f32[64,80,2,64]{1,0,3,2:T(8,128)}, s32[]{:T(128)}, ...), condition=%wide.region_2.0_spmd.clone, body=%wide.region_0.0_spmd.clone.sunk | while | flops 802436160 | bytes 23841520 | solution.py:62
  25.2 8.3 %fusion.32 = bf16[8,8192,64]{1,2,0:T(8,128)(2,1)S(1)} fusion(s32[64]{0:T(128)S(1)} %iota_multiply_fusion.4, s32[8192]{0:T(1024)S(1)} %iota_multiply_fusion.5, s32[8]{0:T(128)S(1)} %select_reduce_fusion.2), kind=kLoop, calls=%fused_computation.10.clone.1 | loop fusion | flops 67108864 | bytes 8421664 | tf_op jit(solution)/shard_map/while/body/eval_jaxpr/convert_element_type | solution.py:52
  33.5 3.7 fusion.33
  37.2 5.1 %bitcast_add_fusion.2 = f32[64,80,2,64]{1,0,3,2:T(8,128)} fusion(f32[64,80,2,64]{1,0,3,2:T(8,128)} %get-tuple-element.261, pred[]{:T(512)S(6)} %compare.3, f32[80,8,64]{0,2,1:T(8,128)S(1)} %bitcast.32, f32[8,64,2,1]{0,2,1,3:T(2,128)S(1)} %bitcast.33), kind=kOutput, calls=%fused_computation.11.clone.1 | convolution fusion | flops 64225280 | bytes 5410817 | tf_op jit(solution)/shard_map/while/body/eval_jaxpr/rkf,kgh->grhf/dot_general | solution.py:57
  42.3 8.3 %fusion.32 = bf16[8,8192,64]{1,2,0:T(8,128)(2,1)S(1)} fusion(s32[64]{0:T(128)S(1)} %iota_multiply_fusion.4, s32[8192]{0:T(1024)S(1)} %iota_multiply_fusion.5, s32[8]{0:T(128)S(1)} %select_reduce_fusion.2), kind=kLoop, calls=%fused_computation.10.clone.1 | loop fusion | flops 67108864 | bytes 8421664 | tf_op jit(solution)/shard_map/while/body/eval_jaxpr/convert_element_type | solution.py:52
  50.7 3.7 fusion.33
  54.4 6.6 %bitcast_add_fusion.2 = f32[64,80,2,64]{1,0,3,2:T(8,128)} fusion(f32[64,80,2,64]{1,0,3,2:T(8,128)} %get-tuple-element.261, pred[]{:T(512)S(6)} %compare.3, f32[80,8,64]{0,2,1:T(8,128)S(1)} %bitcast.32, f32[8,64,2,1]{0,2,1,3:T(2,128)S(1)} %bitcast.33), kind=kOutput, calls=%fused_computation.11.clone.1 | convolution fusion | flops 64225280 | bytes 5410817 | tf_op jit(solution)/shard_map/while/body/eval_jaxpr/rkf,kgh->grhf/dot_general | solution.py:57
  61.1 8.3 %fusion.32 = bf16[8,8192,64]{1,2,0:T(8,128)(2,1)S(1)} fusion(s32[64]{0:T(128)S(1)} %iota_multiply_fusion.4, s32[8192]{0:T(1024)S(1)} %iota_multiply_fusion.5, s32[8]{0:T(128)S(1)} %select_reduce_fusion.2), kind=kLoop, calls=%fused_computation.10.clone.1 | loop fusion | flops 67108864 | bytes 8421664 | tf_op jit(solution)/shard_map/while/body/eval_jaxpr/convert_element_type | solution.py:52
  69.4 3.7 fusion.33
  73.1 6.6 %bitcast_add_fusion.2 = f32[64,80,2,64]{1,0,3,2:T(8,128)} fusion(f32[64,80,2,64]{1,0,3,2:T(8,128)} %get-tuple-element.261, pred[]{:T(512)S(6)} %compare.3, f32[80,8,64]{0,2,1:T(8,128)S(1)} %bitcast.32, f32[8,64,2,1]{0,2,1,3:T(2,128)S(1)} %bitcast.33), kind=kOutput, calls=%fused_computation.11.clone.1 | convolution fusion | flops 64225280 | bytes 5410817 | tf_op jit(solution)/shard_map/while/body/eval_jaxpr/rkf,kgh->grhf/dot_general | solution.py:57
  79.8 8.3 %fusion.32 = bf16[8,8192,64]{1,2,0:T(8,128)(2,1)S(1)} fusion(s32[64]{0:T(128)S(1)} %iota_multiply_fusion.4, s32[8192]{0:T(1024)S(1)} %iota_multiply_fusion.5, s32[8]{0:T(128)S(1)} %select_reduce_fusion.2), kind=kLoop, calls=%fused_computation.10.clone.1 | loop fusion | flops 67108864 | bytes 8421664 | tf_op jit(solution)/shard_map/while/body/eval_jaxpr/convert_element_type | solution.py:52
  88.1 3.7 fusion.33
  91.8 6.6 %bitcast_add_fusion.2 = f32[64,80,2,64]{1,0,3,2:T(8,128)} fusion(f32[64,80,2,64]{1,0,3,2:T(8,128)} %get-tuple-element.261, pred[]{:T(512)S(6)} %compare.3, f32[80,8,64]{0,2,1:T(8,128)S(1)} %bitcast.32, f32[8,64,2,1]{0,2,1,3:T(2,128)S(1)} %bitcast.33), kind=kOutput, calls=%fused_computation.11.clone.1 | convolution fusion | flops 64225280 | bytes 5410817 | tf_op jit(solution)/shard_map/while/body/eval_jaxpr/rkf,kgh->grhf/dot_general | solution.py:57
  98.5 8.3 %fusion.32 = bf16[8,8192,64]{1,2,0:T(8,128)(2,1)S(1)} fusion(s32[64]{0:T(128)S(1)} %iota_multiply_fusion.4, s32[8192]{0:T(1024)S(1)} %iota_multiply_fusion.5, s32[8]{0:T(128)S(1)} %select_reduce_fusion.2), kind=kLoop, calls=%fused_computation.10.clone.1 | loop fusion | flops 67108864 | bytes 8421664 | tf_op jit(solution)/shard_map/while/body/eval_jaxpr/convert_element_type | solution.py:52
  106.9 3.7 fusion.33
  110.6 6.6 %bitcast_add_fusion.2 = f32[64,80,2,64]{1,0,3,2:T(8,128)} fusion(f32[64,80,2,64]{1,0,3,2:T(8,128)} %get-tuple-element.261, pred[]{:T(512)S(6)} %compare.3, f32[80,8,64]{0,2,1:T(8,128)S(1)} %bitcast.32, f32[8,64,2,1]{0,2,1,3:T(2,128)S(1)} %bitcast.33), kind=kOutput, calls=%fused_computation.11.clone.1 | convolution fusion | flops 64225280 | bytes 5410817 | tf_op jit(solution)/shard_map/while/body/eval_jaxpr/rkf,kgh->grhf/dot_general | solution.py:57
  117.3 8.3 %fusion.32 = bf16[8,8192,64]{1,2,0:T(8,128)(2,1)S(1)} fusion(s32[64]{0:T(128)S(1)} %iota_multiply_fusion.4, s32[8192]{0:T(1024)S(1)} %iota_multiply_fusion.5, s32[8]{0:T(128)S(1)} %select_reduce_fusion.2), kind=kLoop, calls=%fused_computation.10.clone.1 | loop fusion | flops 67108864 | bytes 8421664 | tf_op jit(solution)/shard_map/while/body/eval_jaxpr/convert_element_type | solution.py:52
  125.6 3.7 fusion.33
  129.3 6.6 %bitcast_add_fusion.2 = f32[64,80,2,64]{1,0,3,2:T(8,128)} fusion(f32[64,80,2,64]{1,0,3,2:T(8,128)} %get-tuple-element.261, pred[]{:T(512)S(6)} %compare.3, f32[80,8,64]{0,2,1:T(8,128)S(1)} %bitcast.32, f32[8,64,2,1]{0,2,1,3:T(2,128)S(1)} %bitcast.33), kind=kOutput, calls=%fused_computation.11.clone.1 | convolution fusion | flops 64225280 | bytes 5410817 | tf_op jit(solution)/shard_map/while/body/eval_jaxpr/rkf,kgh->grhf/dot_general | solution.py:57
  136.0 8.3 %fusion.32 = bf16[8,8192,64]{1,2,0:T(8,128)(2,1)S(1)} fusion(s32[64]{0:T(128)S(1)} %iota_multiply_fusion.4, s32[8192]{0:T(1024)S(1)} %iota_multiply_fusion.5, s32[8]{0:T(128)S(1)} %select_reduce_fusion.2), kind=kLoop, calls=%fused_computation.10.clone.1 | loop fusion | flops 67108864 | bytes 8421664 | tf_op jit(solution)/shard_map/while/body/eval_jaxpr/convert_element_type | solution.py:52
  144.3 3.7 fusion.33
  148.0 6.6 %bitcast_add_fusion.2 = f32[64,80,2,64]{1,0,3,2:T(8,128)} fusion(f32[64,80,2,64]{1,0,3,2:T(8,128)} %get-tuple-element.261, pred[]{:T(512)S(6)} %compare.3, f32[80,8,64]{0,2,1:T(8,128)S(1)} %bitcast.32, f32[8,64,2,1]{0,2,1,3:T(2,128)S(1)} %bitcast.33), kind=kOutput, calls=%fused_computation.11.clone.1 | convolution fusion | flops 64225280 | bytes 5410817 | tf_op jit(solution)/shard_map/while/body/eval_jaxpr/rkf,kgh->grhf/dot_general | solution.py:57
  154.7 8.3 %fusion.32 = bf16[8,8192,64]{1,2,0:T(8,128)(2,1)S(1)} fusion(s32[64]{0:T(128)S(1)} %iota_multiply_fusion.4, s32[8192]{0:T(1024)S(1)} %iota_multiply_fusion.5, s32[8]{0:T(128)S(1)} %select_reduce_fusion.2), kind=kLoop, calls=%fused_computation.10.clone.1 | loop fusion | flops 67108864 | bytes 8421664 | tf_op jit(solution)/shard_map/while/body/eval_jaxpr/convert_element_type | solution.py:52
  163.1 3.7 fusion.33
  166.8 6.6 %bitcast_add_fusion.2 = f32[64,80,2,64]{1,0,3,2:T(8,128)} fusion(f32[64,80,2,64]{1,0,3,2:T(8,128)} %get-tuple-element.261, pred[]{:T(512)S(6)} %compare.3, f32[80,8,64]{0,2,1:T(8,128)S(1)} %bitcast.32, f32[8,64,2,1]{0,2,1,3:T(2,128)S(1)} %bitcast.33), kind=kOutput, calls=%fused_computation.11.clone.1 | convolution fusion | flops 64225280 | bytes 5410817 | tf_op jit(solution)/shard_map/while/body/eval_jaxpr/rkf,kgh->grhf/dot_general | solution.py:57
  173.4 5.2 %copy.19 = f32[64,80,128]{2,1,0:T(8,128)} copy(f32[64,80,128]{1,0,2:T(8,128)} %bitcast.31) | data formatting | bytes 5242880 | tf_op jit(solution)/shard_map/reshape | solution.py:64
  178.6 0.0 reduce-scatter.2.cloned.1.call-update
  178.6 79.4 %reduce-scatter.2.cloned.1.call-done = f32[4,80,128]{2,1,0:T(8,128)} async-done(((f32[64,80,128]{2,1,0:T(8,128)}), f32[4,80,128]{2,1,0:T(8,128)}) %reduce-scatter.2.cloned.1.call-update) | async-done | bytes 163856 | tf_op jit(solution)/shard_map/reduce_scatter | solution.py:63
  258.0 0.9 multiply_reduce_fusion.1
  258.9 32.8 %psum.21 = f32[16]{0:T(128)S(1)} all-reduce(f32[16]{0:T(128)S(1)} %multiply_reduce_fusion.1), channel_id=1, replica_groups=mesh['feat'=16,'cand'=16] {'feat'}, use_global_device_ids=true, to_apply=%region_5.0 | all-reduce | flops 16 | bytes 128 | tf_op jit(solution)/shard_map/psum | solution.py:68
  291.7 0.8 slice_divide_fusion
  292.5 25.5 %all_gather.3 = f32[4,256,128]{2,1,0:T(8,128)S(1)} all-gather(f32[4,16,128]{2,1,0:T(8,128)S(1)} %slice_divide_fusion), channel_id=1, replica_groups=mesh['feat'=16,'cand'=16] {'cand'}, dimensions={1}, use_global_device_ids=true | all-gather | bytes 557056 | tf_op jit(solution)/shard_map/all_gather | solution.py:70
  318.0 1.5 fusion.18
  319.5 0.1 reduce_sum.44
  319.6 1.0 multiply_reduce_fusion
  320.6 59.9 %all-reduce = (f32[64,64]{0,1:T(8,128)S(1)}, f32[64]{0:T(128)S(1)}) all-reduce(f32[64,64]{0,1:T(8,128)S(1)} %broadcast_multiply_fusion.1, f32[64]{0:T(128)S(1)} %multiply_reduce_fusion), channel_id=1, replica_groups=mesh['feat'=16,'cand'=16] {'feat'}, use_global_device_ids=true, to_apply=%region_7.0 | all-reduce | flops 4160 | bytes 33280 | tf_op jit(solution)/shard_map/psum | solution.py:73
  380.6 0.6 dynamic-slice_divide_fusion
  (36 shorter events, 0.5 us)
Async XLA Ops:
  6.5 12.2 %copy-start = (bf16[16,65536]{1,0:T(8,128)(2,1)S(1)}, bf16[16,65536]{1,0:T(8,128)(2,1)}, u32[]{:S(2)}) copy-start(bf16[16,65536]{1,0:T(8,128)(2,1)} %param.8) | copy-start | bytes 6291460
  6.5 251.5 %reduce-scatter.2.cloned.1.call-start = ((), (), s32[]{:S(2)}) async-start(), calls=%async_computation.1 | async-start | bytes 2785280 | tf_op jit(solution)/shard_map/reduce_scatter | solution.py:63
Sparse Core Ops, SparseCore 0:
  178.7 79.2 reduce-scatter.1
where the time goes:
time: 389 us; the launch traced here: 388 us
  blocking collectives  118 us (30%)
  other arithmetic  87.5 us (22%)
  matrix products  82.5 us (21%)
  waiting for transfers between devices  79.4 us (20%)
  between operations  13.4 us (3%)
  local copies, waits for them, and re-layouts  6.73 us (2%)
    reduce_scatter x1, waiting for transfers between devices, body(): lax.psum_scatter(summed.reshape(groups, height, 128), 'feat', scatter_dim...  79.4 us
    convert_element_type x8, other arithmetic, one_block(): matrices = (jax.vmap(signs_for)(seeds_now) * factor).astype(jnp.bfloat16)  66.6 us
    psum x1, blocking collectives, body(): total = lax.psum(tile, 'feat')  59.9 us
    dot_general x8, matrix products, one_block(): jnp.einsum('rkf,kgh->grhf', partial_out, placing, precision=lax.Precision...  51.4 us
    psum x1, blocking collectives, body(): cand_sq, val_sq = lax.psum((squares(cand_part), squares(val_part)), 'feat')  32.8 us
    while x8, matrix products  29.6 us
    all_gather x1, blocking collectives, body(): val_all = lax.all_gather(val_unit, 'cand', axis=1, tiled=True)  25.5 us
    convert_element_type x1, other arithmetic, body(): adam_grads = (wide / (jnp.sqrt(0.999 * second_moment[None, :] + 0.001 * w...  9.5 us
  transfers between devices with their start and end apart: 1, of which 1 were waited for; matrix products, arithmetic and copies ran while one was open for 0% of the time, Pallas kernels for 0%

commit v1 on v0

v1 whole, which is shorter than its diff:
```python
import math

import jax
import jax.numpy as jnp
import numpy as np
from jax import lax
from jax.experimental import pallas as pl
from jax.experimental.pallas import tpu as pltpu
from jax.sharding import PartitionSpec as P

PB = 8192
FEATS = 8192
FB = 64
SLOTS = 8
VPT = 4
CHUNK = 1024


def wrap32(value):
    value &= 0xFFFFFFFF
    return np.int32(value - (1 << 32) if value >= (1 << 31) else value)


MIX = 73244475
ROW_MUL = wrap32(73856093)
COL_MUL = wrap32(19349663)
MIX_A = wrap32(MIX)
MIX_B = wrap32((MIX << 15) + (1 << 31))


def fold(value):
    return value ^ lax.shift_right_logical(value, jnp.int32(16))


def project(slots, adam, seeds_ref, pos_ref, *refs):
    if adam:
        cand_ref, val_ref, moment_ref, out_ref, rows_ref, acc_ref, across_ref, column_ref = refs
    else:
        rows_ref, out_ref, acc_ref, across_ref, column_ref = refs
    step = pl.program_id(0)
    count = len(slots)
    height = rows_ref.shape[0]

    @pl.when(step == 0)
    def _():
        across = lax.broadcasted_iota(jnp.int32, (8, PB), 1) * ROW_MUL
        across_ref[...] = fold(across)
        column = lax.broadcasted_iota(jnp.int32, (FB, 128), 0) * COL_MUL
        column_ref[...] = fold(column)

    mixed = []
    for slot in slots:
        mixed.append(column_ref[...] ^ fold(seeds_ref[slot, step]))
    mixed = jnp.concatenate(mixed, axis=0)

    def one_chunk(chunk, acc):
        at = pl.ds(pl.multiple_of(chunk * CHUNK, CHUNK), CHUNK)
        if adam:
            wide = cand_ref[:, at].astype(jnp.float32)
            moment = 0.999 * moment_ref[:, at]
            square = moment + (0.001 * wide) * wide
            root = lax.rsqrt(square)
            den = square * root + 1e-08
            inverse = root * (2.0 - den * root)
            ncand = cand_ref.shape[0]
            rows_ref[:ncand, at] = (wide * inverse).astype(jnp.bfloat16)
            rows_ref[ncand:, at] = val_ref[:, at]
        across = across_ref[:, at]
        across = jnp.broadcast_to(across[None], (8 * count, 8, CHUNK)).reshape(FB * count, CHUNK)
        value = across ^ jnp.concatenate([mixed] * (CHUNK // 128), axis=1)
        value = fold(value * MIX_A) * MIX_B
        signs = jnp.where(value < 0, jnp.bfloat16(1.0), jnp.bfloat16(-1.0))
        return acc + lax.dot_general(
            signs,
            rows_ref[:, at],
            (((1,), (1,)), ((), ())),
            preferred_element_type=jnp.float32,
        )

    acc = lax.fori_loop(0, PB // CHUNK, one_chunk, jnp.zeros((FB * count, height), jnp.float32))
    for n, slot in enumerate(slots):
        at = pl.multiple_of(pos_ref[slot, step] * FB, FB)
        acc_ref[n, pl.ds(at, FB), :] = acc[n * FB : (n + 1) * FB]

    @pl.when(step == pl.num_programs(0) - 1)
    def _():
        for n in range(count):
            out_ref[n] = acc_ref[n].T


def projected(slots, seeds, pos, operands, adam):
    count = len(slots)
    if adam:
        cand, val, moment = operands
        height = cand.shape[0] + val.shape[0]
        length = cand.shape[1]
        in_specs = [
            pl.BlockSpec((cand.shape[0], PB), lambda i, *_: (0, i)),
            pl.BlockSpec((val.shape[0], PB), lambda i, *_: (0, i)),
            pl.BlockSpec((1, PB), lambda i, *_: (0, i)),
        ]
    else:
        (rows,) = operands
        height, length = rows.shape
        in_specs = [pl.BlockSpec((height, PB), lambda i, *_: (0, i))]
    blocks = length // PB
    width = blocks * FB
    out_shape = [jax.ShapeDtypeStruct((count, height, width), jnp.float32)]
    out_specs = [pl.BlockSpec((count, height, width), lambda i, *_: (0, 0, 0))]
    if adam:
        out_shape.append(jax.ShapeDtypeStruct((height, length), jnp.bfloat16))
        out_specs.append(pl.BlockSpec((height, PB), lambda i, *_: (0, i)))
    return pl.pallas_call(
        lambda *refs: project(slots, adam, *refs),
        out_shape=out_shape,
        grid_spec=pltpu.PrefetchScalarGridSpec(
            num_scalar_prefetch=2,
            grid=(blocks,),
            in_specs=in_specs,
            out_specs=out_specs,
            scratch_shapes=[
                pltpu.VMEM((count, width, height), jnp.float32),
                pltpu.VMEM((8, PB), jnp.int32),
                pltpu.VMEM((FB, 128), jnp.int32),
            ],
        ),
        compiler_params=pltpu.CompilerParams(vmem_limit_bytes=40 << 20),
        cost_estimate=pl.CostEstimate(
            flops=2 * count * width * height * PB * 16,
            bytes_accessed=2 * height * length,
            transcendentals=0,
        ),
        name="project",
    )(seeds, pos, *operands)


def dots_kernel(cand_ref, val_ref, out_ref):
    cand = cand_ref[...]
    val = val_ref[...]
    last = (((1,), (1,)), ((), ()))
    ncand = cand.shape[0]
    dots = lax.dot_general(
        val, cand, last, precision=lax.Precision.HIGHEST, preferred_element_type=jnp.float32
    )
    val_sq = jnp.sum(val * val, axis=1, keepdims=True)
    cand_sq = lax.dot_general(
        jnp.ones((8, cand.shape[1]), jnp.float32),
        cand * cand,
        last,
        precision=lax.Precision.HIGHEST,
        preferred_element_type=jnp.float32,
    )
    shards, _, lanes = out_ref.shape
    own = val.shape[0] // shards
    both = jnp.concatenate([dots, jnp.broadcast_to(val_sq, (val.shape[0], lanes - ncand))], axis=1)
    out_ref[:, :own, :] = both.reshape(shards, own, lanes)
    squares = jnp.concatenate([cand_sq, jnp.zeros((8, lanes - ncand), jnp.float32)], axis=1)
    for shard in range(shards):
        out_ref[shard, own:, :] = squares


def score_kernel(parts_ref, out_ref):
    ncand, ntask = out_ref.shape
    own = ntask * VPT
    total = jnp.sum(parts_ref[...], axis=0)
    val_norm = jnp.sqrt(total[:own, ncand : ncand + 1] + 1e-06)
    cand_norm = jnp.sqrt(total[own : own + 1, :ncand] + 1e-06)
    cosine = total[:own, :ncand] / val_norm / cand_norm
    row = lax.broadcasted_iota(jnp.int32, (own, ntask), 0)
    task = lax.broadcasted_iota(jnp.int32, (own, ntask), 1)
    mean = jnp.where(row // VPT == task, 1.0 / VPT, 0.0)
    out_ref[...] = lax.dot_general(
        cosine,
        mean,
        (((0,), (0,)), ((), ())),
        precision=lax.Precision.HIGHEST,
        preferred_element_type=jnp.float32,
    )


def body(cand_grads, val_grads, second_moment, slot_blocks, slot_seeds):
    devices = lax.axis_size("feat")
    groups = lax.axis_size("cand")
    blocks = second_moment.shape[0] // PB
    first_block = lax.axis_index("feat") * blocks
    factor = 1.0 / math.sqrt(SLOTS * PB)
    stride = devices // SLOTS
    ncand = cand_grads.shape[0]
    nval = val_grads.shape[0]

    local = first_block + lax.broadcasted_iota(jnp.int32, (1, blocks, 1), 1)
    matches = slot_blocks[:, None, :] == local
    seeds = jnp.sum(jnp.where(matches, slot_seeds[:, None, :], 0), axis=2)
    places = lax.broadcasted_iota(jnp.int32, (1, 1, slot_blocks.shape[1]), 2) % blocks
    pos = jnp.sum(jnp.where(matches, places, 0), axis=2)

    def send(part, slot):
        offset = slot * stride if slot % 2 == 0 else (slot - 1) * stride + 1
        pairs = [(j, (j - offset) % devices) for j in range(devices)]
        return lax.ppermute(part, "feat", pairs)

    order = [(4, 5), (2, 3), (6, 7), (1,), (0,)]
    rows = None
    terms = []
    for slots in order:
        if rows is None:
            operands = (cand_grads, val_grads, second_moment[None, :])
            parts, rows = projected(slots, seeds, pos, operands, True)
        else:
            (parts,) = projected(slots, seeds, pos, (rows,), False)
        for n, slot in enumerate(slots):
            terms.append(send(parts[n], slot) if slot else parts[n])
    mine = sum(terms) * factor
    cand_part = mine[:ncand]
    val_part = mine[ncand:]
    val_all = lax.all_to_all(
        jnp.broadcast_to(val_part[None], (groups, *val_part.shape)), "cand", 0, 0, tiled=True
    )
    val_all = val_all.reshape(groups * nval, val_part.shape[1])
    own = groups * nval // devices
    packed = pl.pallas_call(
        dots_kernel,
        out_shape=jax.ShapeDtypeStruct((devices, own + 8, 128), jnp.float32),
        name="dots",
    )(cand_part, val_all)
    parts = lax.all_to_all(packed, "feat", 0, 0, tiled=True)
    return pl.pallas_call(
        score_kernel,
        out_shape=jax.ShapeDtypeStruct((ncand, own // VPT), jnp.float32),
        name="score",
    )(parts)


def solution(mesh):
    placed = (P("cand", "feat"), P("cand", "feat"), P("feat"), P(), P())
    return jax.shard_map(
        body, mesh=mesh, in_specs=placed, out_specs=P("cand", "feat"), check_vma=False
    )
```

time: 389 us -> 164 us (0.42)
  blocking collectives: 118 us -> 16 us
  Pallas kernels: 0 us -> 93.9 us
  other arithmetic: 87.5 us -> 1.24 us
  matrix products: 82.5 us -> 0 us
  waiting for transfers between devices: 79.4 us -> 11.7 us
  starting transfers between devices: 0.01 us -> 25.8 us
  between operations: 13.4 us -> 0.16 us
  local copies, waits for them, and re-layouts: 6.73 us -> 13.7 us
    pallas_call x0 -> x7, Pallas kernels: none -> 93.9 us  [the longest x5 89.6 us: projected(): pl.pallas_call(lambda *refs: project(slots, adam, *refs), out_shape=out_s...]
    psum x2 -> x0, blocking collectives: 92.7 us -> none  [the longest x1 59.9 us: body(): total = lax.psum(tile, 'feat')]
    reduce_scatter x1 -> x0, waiting for transfers between devices: 79.4 us -> none  [body(): lax.psum_scatter(summed.reshape(groups, height, 128), 'feat', scatter_dim...]
    convert_element_type x17 -> x0, other arithmetic: 76.2 us -> none  [the longest x8 66.6 us: one_block(): matrices = (jax.vmap(signs_for)(seeds_now) * factor).astype(jnp.bfloat16)]
    dot_general x9 -> x0, matrix products: 52.9 us -> none  [the longest x8 51.4 us: one_block(): jnp.einsum('rkf,kgh->grhf', partial_out, placing, precision=lax.Precision...]
    while x8 -> x0, matrix products: 29.6 us -> none
    all_gather x1 -> x0, blocking collectives: 25.5 us -> none  [body(): val_all = lax.all_gather(val_unit, 'cand', axis=1, tiled=True)]
    ppermute x0 -> x7, starting transfers between devices: none -> 18.8 us  [send(): return lax.ppermute(part, 'feat', pairs)]
  transfers between devices with their start and end apart: 1 -> 8, of which waited for: 1 -> 1; matrix products, arithmetic and copies ran while one was open for 0% -> 0% of each run, Pallas kernels for 0% -> 31%
where the time goes in v1:
time: 164 us; the launch traced here: 162 us
  Pallas kernels  93.9 us (57%)
  starting transfers between devices  25.8 us (16%)
  blocking collectives  16 us (10%)
  local copies, waits for them, and re-layouts  13.7 us (8%)
  waiting for transfers between devices  11.7 us (7%)
    pallas_call x5, Pallas kernels, projected(): pl.pallas_call(lambda *refs: project(slots, adam, *refs), out_shape=out_s...  89.6 us
    ppermute x7, starting transfers between devices, send(): return lax.ppermute(part, 'feat', pairs)  18.8 us
    all_to_all x1, blocking collectives, body(): parts = lax.all_to_all(packed, 'feat', 0, 0, tiled=True)  16 us
    all_to_all x1, waiting for transfers between devices, body(): lax.all_to_all(jnp.broadcast_to(val_part[None], (groups, *val_part.shape)...  11.7 us
    unnamed x10, local copies, waits for them, and re-layouts  10.7 us
    all_to_all x1, starting transfers between devices, body(): lax.all_to_all(jnp.broadcast_to(val_part[None], (groups, *val_part.shape)...  7.03 us
  transfers between devices with their start and end apart: 8, of which 1 were waited for; matrix products, arithmetic and copies ran while one was open for 0% of the time, Pallas kernels for 31%

profile of v1, /device:TPU:0, one launch (start us, length us, event | category | flops | bytes accessed | tf_op | source)
XLA Modules:
  0.0 162.5 jit_solution(11074884374533011066)
XLA Ops:
  0.0 1.1 fusion.2
  1.1 0.0 copy-start
  1.1 3.4 %copy-done = bf16[64,65536]{1,0:T(8,128)(2,1)S(1)} copy-done((bf16[64,65536]{1,0:T(8,128)(2,1)S(1)}, bf16[64,65536]{1,0:T(8,128)(2,1)}, u32[]{:S(2)}) %copy-start) | copy-done | bytes 8388632
  4.5 0.0 copy-start.1
  4.5 1.6 copy-done.1
  6.1 0.0 copy-start.2
  6.1 0.9 copy-done.2
  7.1 24.6 %project.5 = (f32[2,80,512]{2,1,0:T(8,128)S(1)}, bf16[80,65536]{1,0:T(8,128)(2,1)}) custom-call(s32[8,8]{1,0:T(8,128)S(1)} %get-tuple-element.10.refs_0_, s32[8,8]{1,0:T(8,128)S(1)} %get-tuple-element.9.refs_1_, bf16[64,65536]{1,0:T(8,128)(2,1)S(1)} %copy-done, bf16[16,65536]{1,0:T(8,128)(2,1)S(1)} %copy-done.1, f32[1,65536]{1,0:T(1,128)S(1)} %bitcast.19), custom_call_target="tpu_custom_call" | custom-call | flops 21474836480 | bytes 10485760 | tf_op jit(solution)/shard_map/project/pallas_call | solution.py:113
  31.6 0.0 copy-start.3
  31.6 4.0 %copy-done.3 = bf16[80,65536]{1,0:T(8,128)(2,1)S(1)} copy-done((bf16[80,65536]{1,0:T(8,128)(2,1)S(1)}, bf16[80,65536]{1,0:T(8,128)(2,1)}, u32[]{:S(2)}) %copy-start.3) | copy-done | bytes 10485784
  35.6 14.4 %project.8 = f32[1,80,512]{2,1,0:T(8,128)S(1)} custom-call(s32[8,8]{1,0:T(8,128)S(1)} %get-tuple-element.10.refs_0_, s32[8,8]{1,0:T(8,128)S(1)} %get-tuple-element.9.refs_1_, bf16[80,65536]{1,0:T(8,128)(2,1)S(1)} %copy-done.3), custom_call_target="tpu_custom_call" | custom-call | flops 10737418240 | bytes 10485760 | tf_op jit(solution)/shard_map/project/pallas_call | solution.py:113
  50.0 5.2 %collective-permute-start.6 = (f32[80,512]{1,0:T(8,128)S(1)}, f32[80,512]{1,0:T(8,128)S(1)}, u32[]{:S(2)}, u32[]{:S(2)}) collective-permute-start(f32[80,512]{1,0:T(8,128)S(1)} %bitcast.20), channel_id=1, source_target_pairs={{0,240},{16,0},{32,16},{48,32},{64,48},{80,64},{96,80},{112,96},{1... | collective-permute-start | bytes 491528 | tf_op jit(solution)/shard_map/ppermute | solution.py:200
  55.3 0.1 collective-permute-start.1
  55.4 3.7 %collective-permute-start = (f32[80,512]{1,0:T(8,128)S(1)}, f32[80,512]{1,0:T(8,128)S(1)}, u32[]{:S(2)}, u32[]{:S(2)}) collective-permute-start(f32[80,512]{1,0:T(8,128)S(1)} %get-tuple-element.12), channel_id=1, source_target_pairs={{0,128},{16,144},{32,160},{48,176},{64,192},{80,208},{96,224},{112... | collective-permute-start | bytes 491528 | tf_op jit(solution)/shard_map/ppermute | solution.py:200
  59.1 18.1 %project.7 = f32[2,80,512]{2,1,0:T(8,128)S(1)} custom-call(s32[8,8]{1,0:T(8,128)S(1)} %get-tuple-element.10.refs_0_, s32[8,8]{1,0:T(8,128)S(1)} %get-tuple-element.9.refs_1_, bf16[80,65536]{1,0:T(8,128)(2,1)S(1)} %copy-done.3), custom_call_target="tpu_custom_call" | custom-call | flops 21474836480 | bytes 10485760 | tf_op jit(solution)/shard_map/project/pallas_call | solution.py:113
  77.2 0.3 collective-permute-start.4
  77.5 2.4 %collective-permute-start.5 = (f32[80,512]{1,0:T(8,128)S(1)}, f32[80,512]{1,0:T(8,128)S(1)}, u32[]{:S(2)}, u32[]{:S(2)}) collective-permute-start(f32[80,512]{1,0:T(8,128)S(1)} %get-tuple-element.16), channel_id=1, source_target_pairs={{0,48},{16,64},{32,80},{48,96},{64,112},{80,128},{96,144},{112,160... | collective-permute-start | bytes 491528 | tf_op jit(solution)/shard_map/ppermute | solution.py:200
  79.9 18.1 %project.6 = f32[2,80,512]{2,1,0:T(8,128)S(1)} custom-call(s32[8,8]{1,0:T(8,128)S(1)} %get-tuple-element.10.refs_0_, s32[8,8]{1,0:T(8,128)S(1)} %get-tuple-element.9.refs_1_, bf16[80,65536]{1,0:T(8,128)(2,1)S(1)} %copy-done.3), custom_call_target="tpu_custom_call" | custom-call | flops 21474836480 | bytes 10485760 | tf_op jit(solution)/shard_map/project/pallas_call | solution.py:113
  98.0 0.0 collective-permute-done.6
  98.1 3.2 %collective-permute-start.2 = (f32[80,512]{1,0:T(8,128)S(1)}, f32[80,512]{1,0:T(8,128)S(1)}, u32[]{:S(2)}, u32[]{:S(2)}) collective-permute-start(f32[80,512]{1,0:T(8,128)S(1)} %get-tuple-element.13), channel_id=1, source_target_pairs={{0,192},{16,208},{32,224},{48,240},{64,0},{80,16},{96,32},{112,48}... | collective-permute-start | bytes 491528 | tf_op jit(solution)/shard_map/ppermute | solution.py:200
  101.3 0.0 collective-permute-done.1
  101.3 3.9 %collective-permute-start.3 = (f32[80,512]{1,0:T(8,128)S(1)}, f32[80,512]{1,0:T(8,128)S(1)}, u32[]{:S(2)}, u32[]{:S(2)}) collective-permute-start(f32[80,512]{1,0:T(8,128)S(1)} %get-tuple-element.14), channel_id=1, source_target_pairs={{0,176},{16,192},{32,208},{48,224},{64,240},{80,0},{96,16},{112,32... | collective-permute-start | bytes 491528 | tf_op jit(solution)/shard_map/ppermute | solution.py:200
  105.2 14.4 %project.9 = f32[1,80,512]{2,1,0:T(8,128)S(1)} custom-call(s32[8,8]{1,0:T(8,128)S(1)} %get-tuple-element.10.refs_0_, s32[8,8]{1,0:T(8,128)S(1)} %get-tuple-element.9.refs_1_, bf16[80,65536]{1,0:T(8,128)(2,1)S(1)} %copy-done.3), custom_call_target="tpu_custom_call" | custom-call | flops 10737418240 | bytes 10485760 | tf_op jit(solution)/shard_map/project/pallas_call | solution.py:113
  119.6 0.0 collective-permute-done
  119.6 0.0 collective-permute-done.4
  119.6 0.0 collective-permute-done.5
  119.6 0.0 collective-permute-done.2
  119.6 0.0 collective-permute-done.3
  119.6 0.1 fusion
  119.8 0.9 broadcast_in_dim.37
  120.6 7.0 %all-to-all-start = ((f32[16,16,512]{2,1,0:T(8,128)}), f32[16,16,512]{2,1,0:T(8,128)S(1)}, u32[]{:S(2)}, u32[]{:S(2)}) async-start(f32[16,16,512]{2,1,0:T(8,128)} %broadcast_in_dim.37), calls=%async_computation | async-start | bytes 1048576 | tf_op jit(solution)/shard_map/all_to_all | solution.py:216
  127.6 0.7 slice.36.cand_ref
  128.3 11.7 %all-to-all-done = f32[16,16,512]{2,1,0:T(8,128)S(1)} async-done(((f32[16,16,512]{2,1,0:T(8,128)}), f32[16,16,512]{2,1,0:T(8,128)S(1)}, u32[]{:S(2)}, u32[]{:S(2)}) %all-to-all-start) | async-done | bytes 524320 | tf_op jit(solution)/shard_map/all_to_all | solution.py:216
  140.0 0.0 copy-start.4
  140.0 0.8 copy-done.4
  140.8 2.5 %dots.1 = f32[16,24,128]{2,1,0:T(8,128)} custom-call(f32[64,512]{1,0:T(8,128)} %slice.36.cand_ref, f32[256,512]{1,0:T(8,128)} %bitcast.21), custom_call_target="tpu_custom_call" | custom-call | tf_op jit(solution)/shard_map/dots/pallas_call | solution.py:221
  143.2 16.0 %all_to_all.10.parts_ref = f32[16,24,128]{2,1,0:T(8,128)} all-to-all(f32[16,24,128]{2,1,0:T(8,128)} %dots.1), channel_id=1, replica_groups=mesh['feat'=16,'cand'=16] {'feat'}, dimensions={0} | all-to-all | bytes 393216 | tf_op jit(solution)/shard_map/all_to_all | solution.py:226
  159.2 1.9 %score.1 = f32[64,4]{1,0:T(8,128)} custom-call(f32[16,24,128]{2,1,0:T(8,128)} %all_to_all.10.parts_ref), custom_call_target="tpu_custom_call" | custom-call | tf_op jit(solution)/shard_map/score/pallas_call | solution.py:227
  161.1 1.4 copy.7
  (6 shorter events, 0.1 us)
Async XLA Ops:
  1.1 3.4 %copy-start = (bf16[64,65536]{1,0:T(8,128)(2,1)S(1)}, bf16[64,65536]{1,0:T(8,128)(2,1)}, u32[]{:S(2)}) copy-start(bf16[64,65536]{1,0:T(8,128)(2,1)} %refs_2_.1) | copy-start | bytes 25165828
  4.5 1.6 copy-start.1
  6.1 0.9 copy-start.2
  31.6 4.0 %copy-start.3 = (bf16[80,65536]{1,0:T(8,128)(2,1)S(1)}, bf16[80,65536]{1,0:T(8,128)(2,1)}, u32[]{:S(2)}) copy-start(bf16[80,65536]{1,0:T(8,128)(2,1)} %get-tuple-element.8.refs_2_) | copy-start | bytes 31457284
  50.0 48.0 %collective-permute-start.6 = (f32[80,512]{1,0:T(8,128)S(1)}, f32[80,512]{1,0:T(8,128)S(1)}, u32[]{:S(2)}, u32[]{:S(2)}) collective-permute-start(f32[80,512]{1,0:T(8,128)S(1)} %bitcast.20), channel_id=1, source_target_pairs={{0,240},{16,0},{32,16},{48,32},{64,48},{80,64},{96,80},{112,96},{1... | collective-permute-start | bytes 491528 | tf_op jit(solution)/shard_map/ppermute | solution.py:200
  55.3 46.0 %collective-permute-start.1 = (f32[80,512]{1,0:T(8,128)S(1)}, f32[80,512]{1,0:T(8,128)S(1)}, u32[]{:S(2)}, u32[]{:S(2)}) collective-permute-start(f32[80,512]{1,0:T(8,128)S(1)} %get-tuple-element.11), channel_id=1, source_target_pairs={{0,112},{16,128},{32,144},{48,160},{64,176},{80,192},{96,208},{112... | collective-permute-start | bytes 491528 | tf_op jit(solution)/shard_map/ppermute | solution.py:200
  55.4 64.2 %collective-permute-start = (f32[80,512]{1,0:T(8,128)S(1)}, f32[80,512]{1,0:T(8,128)S(1)}, u32[]{:S(2)}, u32[]{:S(2)}) collective-permute-start(f32[80,512]{1,0:T(8,128)S(1)} %get-tuple-element.12), channel_id=1, source_target_pairs={{0,128},{16,144},{32,160},{48,176},{64,192},{80,208},{96,224},{112... | collective-permute-start | bytes 491528 | tf_op jit(solution)/shard_map/ppermute | solution.py:200
  77.2 42.3 %collective-permute-start.4 = (f32[80,512]{1,0:T(8,128)S(1)}, f32[80,512]{1,0:T(8,128)S(1)}, u32[]{:S(2)}, u32[]{:S(2)}) collective-permute-start(f32[80,512]{1,0:T(8,128)S(1)} %get-tuple-element.15), channel_id=1, source_target_pairs={{0,64},{16,80},{32,96},{48,112},{64,128},{80,144},{96,160},{112,17... | collective-permute-start | bytes 491528 | tf_op jit(solution)/shard_map/ppermute | solution.py:200
  77.5 42.1 %collective-permute-start.5 = (f32[80,512]{1,0:T(8,128)S(1)}, f32[80,512]{1,0:T(8,128)S(1)}, u32[]{:S(2)}, u32[]{:S(2)}) collective-permute-start(f32[80,512]{1,0:T(8,128)S(1)} %get-tuple-element.16), channel_id=1, source_target_pairs={{0,48},{16,64},{32,80},{48,96},{64,112},{80,128},{96,144},{112,160... | collective-permute-start | bytes 491528 | tf_op jit(solution)/shard_map/ppermute | solution.py:200
  98.1 21.5 %collective-permute-start.2 = (f32[80,512]{1,0:T(8,128)S(1)}, f32[80,512]{1,0:T(8,128)S(1)}, u32[]{:S(2)}, u32[]{:S(2)}) collective-permute-start(f32[80,512]{1,0:T(8,128)S(1)} %get-tuple-element.13), channel_id=1, source_target_pairs={{0,192},{16,208},{32,224},{48,240},{64,0},{80,16},{96,32},{112,48}... | collective-permute-start | bytes 491528 | tf_op jit(solution)/shard_map/ppermute | solution.py:200
  101.3 18.4 %collective-permute-start.3 = (f32[80,512]{1,0:T(8,128)S(1)}, f32[80,512]{1,0:T(8,128)S(1)}, u32[]{:S(2)}, u32[]{:S(2)}) collective-permute-start(f32[80,512]{1,0:T(8,128)S(1)} %get-tuple-element.14), channel_id=1, source_target_pairs={{0,176},{16,192},{32,208},{48,224},{64,240},{80,0},{96,16},{112,32... | collective-permute-start | bytes 491528 | tf_op jit(solution)/shard_map/ppermute | solution.py:200
  120.6 19.4 %all-to-all-start = ((f32[16,16,512]{2,1,0:T(8,128)}), f32[16,16,512]{2,1,0:T(8,128)S(1)}, u32[]{:S(2)}, u32[]{:S(2)}) async-start(f32[16,16,512]{2,1,0:T(8,128)} %broadcast_in_dim.37), calls=%async_computation | async-start | bytes 1048576 | tf_op jit(solution)/shard_map/all_to_all | solution.py:216
  140.0 0.8 copy-start.4

commit v2 on v1

v2 whole, which is shorter than its diff:
```python
import math

import jax
import jax.numpy as jnp
import numpy as np
from jax import lax
from jax.experimental import pallas as pl
from jax.experimental.pallas import tpu as pltpu
from jax.sharding import PartitionSpec as P


PB = 8192
FB = 64
SLOTS = 8
VPT = 4
GRANT = 62 << 20
AHEAD = 2
ORDER = ((4, 5, 2, 3), (6, 7, 1), (0,))


def wrap32(value):
    value &= 0xFFFFFFFF
    return np.int32(value - (1 << 32) if value >= (1 << 31) else value)


MIX = 73244475
ROW_MUL = wrap32(73856093)
COL_MUL = wrap32(19349663)
MIX_A = wrap32(MIX)
MIX_B = wrap32((MIX << 15) + (1 << 31))


def fold(value):
    return value ^ lax.shift_right_logical(value, jnp.int32(16))


def offset_of(slot, stride):
    return slot * stride if slot % 2 == 0 else (slot - 1) * stride + 1


def project(slots, adam, devices, me_ref, blocks_ref, seeds_ref, *refs):
    if adam:
        cand_hbm, val_hbm, moment_hbm, *out_refs = refs
        *out_refs, rows_hbm, rows_ref, acc_ref, table_ref, sem, cand_ref, moment_ref = out_refs
    else:
        rows_hbm, *out_refs = refs
        *out_refs, rows_ref, acc_ref, table_ref, sem = out_refs
    count = len(slots)
    height, length = rows_ref.shape
    blocks = length // PB

    def copies(block):
        at = pl.ds(pl.multiple_of(block * PB, PB), PB)
        if not adam:
            return (pltpu.make_async_copy(rows_hbm.at[:, at], rows_ref.at[:, at], sem.at[0, block]),)
        ncand = cand_ref.shape[0]
        return (
            pltpu.make_async_copy(moment_hbm.at[:, at], moment_ref.at[:, at], sem.at[0, block]),
            pltpu.make_async_copy(cand_hbm.at[:, at], cand_ref.at[:, at], sem.at[1, block]),
            pltpu.make_async_copy(val_hbm.at[:, at], rows_ref.at[ncand:, at], sem.at[2, block]),
        )

    def copy_out(block):
        at = pl.ds(pl.multiple_of(block * PB, PB), PB)
        return pltpu.make_async_copy(rows_ref.at[:, at], rows_hbm.at[:, at], sem.at[3, block])

    for block in range(AHEAD):
        for copy in copies(block):
            copy.start()
    me = me_ref[0]
    for n, slot in enumerate(slots):
        owner = lax.rem(me + devices - offset_of(slot, devices // SLOTS), devices)
        for place in range(blocks):
            source = blocks_ref[slot, owner * blocks + place] - me * blocks
            table_ref[0, n, source] = seeds_ref[slot, owner * blocks + place]
            table_ref[1, n, source] = place
    across = fold(lax.broadcasted_iota(jnp.int32, (8, PB), 1) * ROW_MUL)
    column = fold(lax.broadcasted_iota(jnp.int32, (FB, 128), 0) * COL_MUL)
    lane_half = lax.broadcasted_iota(jnp.int32, (height, 2 * FB), 1) // FB

    def one_block(block, carry):
        at = pl.ds(pl.multiple_of(block * PB, PB), PB)

        @pl.when(block + AHEAD < blocks)
        def _():
            for copy in copies(block + AHEAD):
                copy.start()

        for copy in copies(block):
            copy.wait()
        if adam:
            wide = cand_ref[:, at].astype(jnp.float32)
            square = 0.999 * moment_ref[:, at] + (0.001 * wide) * wide
            den = square * lax.rsqrt(square) + 1e-08
            rows_ref[: cand_ref.shape[0], at] = (wide * lax.rsqrt(den * den)).astype(jnp.bfloat16)
            copy_out(block).start()
        mixed = []
        for n in range(count):
            mixed.append(column ^ fold(table_ref[0, n, block]))
        mixed = jnp.concatenate(mixed, axis=0)
        value = jnp.broadcast_to(across[None], (8 * count, 8, PB)).reshape(FB * count, PB)
        value = value ^ jnp.concatenate([mixed] * (PB // 128), axis=1)
        value = fold(value * MIX_A) * MIX_B
        signs = jnp.where(value < 0, jnp.bfloat16(1.0), jnp.bfloat16(-1.0))
        acc = lax.dot_general(
            rows_ref[:, at],
            signs,
            (((1,), (1,)), ((), ())),
            preferred_element_type=jnp.float32,
        )
        if count % 2:
            acc = jnp.concatenate([acc, jnp.zeros((height, FB), jnp.float32)], axis=1)
        for n in range(count):
            place = table_ref[1, n, block]
            half = place % 2
            pair = n // 2 * 2 * FB
            moved = pltpu.roll(acc[:, pair : pair + 2 * FB], (half ^ (n % 2)) * FB, 1)
            acc_ref[n, place // 2] = jnp.where(lane_half == half, moved, acc_ref[n, place // 2])
        return carry

    lax.fori_loop(0, blocks, one_block, 0)
    for n in range(count):
        for pair in range(acc_ref.shape[1]):
            out_refs[n][:, pair * 2 * FB : (pair + 1) * 2 * FB] = acc_ref[n, pair]
    if adam:
        for block in range(blocks):
            copy_out(block).wait()


def projected(slots, tables, operands, adam, devices):
    count = len(slots)
    smem = pl.BlockSpec(memory_space=pltpu.SMEM)
    vmem = pl.BlockSpec(memory_space=pltpu.VMEM)
    if adam:
        cand, val, moment = operands
        height = cand.shape[0] + val.shape[0]
        length = cand.shape[1]
    else:
        (rows,) = operands
        height, length = rows.shape
    blocks = length // PB
    width = blocks * FB
    out_shape = [jax.ShapeDtypeStruct((height, width), jnp.float32)] * count
    out_specs = [vmem] * count
    scratch = [
        pltpu.VMEM((height, length), jnp.bfloat16),
        pltpu.VMEM((count, width // (2 * FB), height, 2 * FB), jnp.float32),
        pltpu.SMEM((2, count, blocks), jnp.int32),
        pltpu.SemaphoreType.DMA((4, blocks)),
    ]
    if adam:
        out_shape.append(jax.ShapeDtypeStruct((height, length), jnp.bfloat16))
        out_specs.append(pl.BlockSpec(memory_space=pl.ANY))
        scratch += [
            pltpu.VMEM(cand.shape, jnp.bfloat16),
            pltpu.VMEM(moment.shape, jnp.float32),
        ]
    return pl.pallas_call(
        lambda *refs: project(slots, adam, devices, *refs),
        out_shape=out_shape,
        in_specs=[smem, smem, smem] + [pl.BlockSpec(memory_space=pl.ANY)] * len(operands),
        out_specs=out_specs,
        scratch_shapes=scratch,
        compiler_params=pltpu.CompilerParams(vmem_limit_bytes=GRANT),
        cost_estimate=pl.CostEstimate(
            flops=2 * count * width * height * PB * 16,
            bytes_accessed=2 * height * length,
            transcendentals=0,
        ),
        name="project",
    )(*tables, *operands)


def merge_kernel(*refs):
    *term_refs, cand_ref, val_ref = refs
    total = term_refs[0][...]
    for term_ref in term_refs[1:]:
        total = total + term_ref[...]
    total = total * (1.0 / math.sqrt(SLOTS * PB))
    ncand = cand_ref.shape[0]
    cand_ref[...] = total[:ncand]
    val_ref[...] = jnp.broadcast_to(total[None, ncand:], val_ref.shape)


def dots_kernel(core_ref, cand_ref, own_ref, other_ref, out_ref):
    cand = cand_ref[...]
    last = (((1,), (1,)), ((), ()))
    ncand = cand.shape[0]
    groups, cores, _, lanes = out_ref.shape
    nval = own_ref.shape[1]
    cand_sq = lax.dot_general(
        jnp.ones((8, cand.shape[1]), jnp.float32),
        cand * cand,
        last,
        precision=lax.Precision.HIGHEST,
        preferred_element_type=jnp.float32,
    )
    squares = jnp.concatenate([cand_sq, jnp.zeros((8, lanes - ncand), jnp.float32)], axis=1)
    val = jnp.concatenate(
        [ref[...].reshape(groups * nval, ref.shape[2]) for ref in (own_ref, other_ref)], axis=0
    )
    dots = lax.dot_general(
        val, cand, last, precision=lax.Precision.HIGHEST, preferred_element_type=jnp.float32
    )
    val_sq = jnp.sum(val * val, axis=1, keepdims=True)
    both = jnp.concatenate([dots, jnp.broadcast_to(val_sq, (val.shape[0], lanes - ncand))], axis=1)
    for swapped in range(cores):
        core = core_ref[0] ^ swapped
        for group in range(groups):
            at = (swapped * groups + group) * nval
            out_ref[group, core, :nval, :] = both[at : at + nval]
            out_ref[group, core, nval:, :] = squares


def score_kernel(parts_ref, out_ref):
    ntask, ncand = out_ref.shape
    own = ntask * VPT
    total = jnp.sum(parts_ref[...], axis=0)
    val_norm = jnp.sqrt(total[:own, ncand : ncand + 1] + 1e-06)
    cand_norm = jnp.sqrt(total[own : own + 1, :ncand] + 1e-06)
    cosine = total[:own, :ncand] / val_norm / cand_norm
    rows = [
        jnp.sum(cosine[task * VPT : (task + 1) * VPT], axis=0, keepdims=True) for task in range(ntask)
    ]
    out_ref[...] = jnp.concatenate(rows, axis=0) / VPT


def body(cand_grads, val_grads, second_moment, slot_blocks, slot_seeds):
    devices = lax.axis_size("feat")
    groups = lax.axis_size("cand")
    ncand = cand_grads.shape[0]
    nval = val_grads.shape[0]

    tables = (lax.axis_index("feat").reshape(1), slot_blocks, slot_seeds)

    def send(part, slot):
        offset = offset_of(slot, devices // SLOTS)
        pairs = [(j, (j - offset) % devices) for j in range(devices)]
        return lax.ppermute(part, "feat", pairs)

    rows = None
    terms = []
    for slots in ORDER:
        if rows is None:
            operands = (cand_grads, val_grads, second_moment[None, :])
            *parts, rows = projected(slots, tables, operands, True, devices)
        else:
            parts = projected(slots, tables, (rows,), False, devices)
        for part, slot in zip(parts, slots):
            terms.append(send(part, slot) if slot else part)
    small = pltpu.CompilerParams(vmem_limit_bytes=8 << 20)
    pairs = groups // 2
    width = terms[0].shape[1]
    cand_part, val_part = pl.pallas_call(
        merge_kernel,
        out_shape=[
            jax.ShapeDtypeStruct((ncand, width), jnp.float32),
            jax.ShapeDtypeStruct((pairs, nval, width), jnp.float32),
        ],
        compiler_params=small,
        name="merge",
    )(*terms)
    same_core = [[2 * m + core for m in range(pairs)] for core in range(2)]
    val_own = lax.all_to_all(
        val_part, "cand", 0, 0, tiled=True, axis_index_groups=same_core
    )
    val_other = lax.ppermute(val_own, "cand", [(c, c ^ 1) for c in range(groups)])
    own = groups * nval // devices
    packed = pl.pallas_call(
        dots_kernel,
        out_shape=jax.ShapeDtypeStruct((pairs, 2, own + 8, 128), jnp.float32),
        in_specs=[pl.BlockSpec(memory_space=pltpu.SMEM)] + [pl.BlockSpec()] * 3,
        compiler_params=small,
        name="dots",
    )((lax.axis_index("cand") % 2).reshape(1), cand_part, val_own, val_other)
    packed = packed.reshape(devices, own + 8, 128)
    parts = lax.all_to_all(packed, "feat", 0, 0, tiled=True)
    return pl.pallas_call(
        score_kernel,
        out_shape=jax.ShapeDtypeStruct((own // VPT, ncand), jnp.float32),
        compiler_params=small,
        name="score",
    )(parts).T


def solution(mesh):
    placed = (P("cand", "feat"), P("cand", "feat"), P("feat"), P(), P())
    return jax.shard_map(
        body, mesh=mesh, in_specs=placed, out_specs=P("cand", "feat"), check_vma=False
    )
```

time: 164 us -> 119 us (0.73)
  Pallas kernels: 93.9 us -> 53.3 us
  blocking collectives: 16 us -> 32.5 us
  local copies, waits for them, and re-layouts: 13.7 us -> 0.93 us
  waiting for transfers between devices: 11.7 us -> 5.17 us
    pallas_call x7 -> x6, Pallas kernels: 93.9 us -> 53.3 us  [the longest x3 51.9 us: projected(): pl.pallas_call(lambda *refs: project(slots, adam, devices, *refs), out_sh...]
    all_to_all x0 -> x1, blocking collectives: none -> 15.6 us  [body(): lax.all_to_all(val_part, 'cand', 0, 0, tiled=True, axis_index_groups=same...]
    all_to_all x1 -> x0, waiting for transfers between devices: 11.7 us -> none  [body(): lax.all_to_all(jnp.broadcast_to(val_part[None], (groups, *val_part.shape)...]
    unnamed x10, local copies, waits for them, and re-layouts: 10.7 us -> 0.93 us
    ppermute x7, starting transfers between devices: 18.8 us -> 26.1 us  [send(): return lax.ppermute(part, 'feat', pairs)]
    all_to_all x1 -> x0, starting transfers between devices: 7.03 us -> none  [body(): lax.all_to_all(jnp.broadcast_to(val_part[None], (groups, *val_part.shape)...]
    ppermute x7, waiting for transfers between devices: 0.02 us -> 3.63 us  [send(): return lax.ppermute(part, 'feat', pairs)]
  transfers between devices with their start and end apart: 8 -> 8, of which waited for: 1 -> 4; matrix products, arithmetic and copies ran while one was open for 0% -> 0% of each run, Pallas kernels for 31% -> 8%
where the time goes in v2:
time: 119 us; the launch traced here: 118 us
  Pallas kernels  53.3 us (45%)
  blocking collectives  32.5 us (27%)
  starting transfers between devices  26.1 us (22%)
  waiting for transfers between devices  5.17 us (4%)
    pallas_call x3, Pallas kernels, projected(): pl.pallas_call(lambda *refs: project(slots, adam, devices, *refs), out_sh...  51.9 us
    ppermute x7, starting transfers between devices, send(): return lax.ppermute(part, 'feat', pairs)  26.1 us
    all_to_all x1, blocking collectives, body(): parts = lax.all_to_all(packed, 'feat', 0, 0, tiled=True)  16.9 us
    all_to_all x1, blocking collectives, body(): lax.all_to_all(val_part, 'cand', 0, 0, tiled=True, axis_index_groups=same...  15.6 us
    ppermute x7, waiting for transfers between devices, send(): return lax.ppermute(part, 'feat', pairs)  3.63 us
  transfers between devices with their start and end apart: 8, of which 4 were waited for; matrix products, arithmetic and copies ran while one was open for 0% of the time, Pallas kernels for 8%

profile of v2, /device:TPU:0, one launch (start us, length us, event | category | flops | bytes accessed | tf_op | source)
XLA Modules:
  0.0 118.1 jit_solution(13695630417360772164)
XLA Ops:
  0.0 26.1 %project.3 = (f32[80,512]{1,0:T(8,128)}, f32[80,512]{1,0:T(8,128)}, f32[80,512]{1,0:T(8,128)}, f32[80,512]{1,0:T(8,128)}, bf16[80,65536]{1,0:T(8,128)(2,1)}) custom-call(s32[1]{0:T(128)} %bitcast.1.refs_0_, s32[8,128]{1,0:T(8,128)} %refs_1_.5, s32[8,128]{1,0:T(8,128)} %refs_2_.5, bf16[64,65536]{1,0:T(8,128)(2,1)} %refs_3_.1, bf16[16,65536]{1,0:T(8,128)(2,1)} %refs_4_.1, ...), custom_call_target="tpu_custom_call" | custom-call | flops 42949672960 | bytes 10485760 | tf_op jit(solution)/shard_map/project/pallas_call | solution.py:158
  26.1 0.0 copy-start.4
  26.1 0.0 copy-start.3
  26.1 0.0 copy-start.2
  26.1 0.0 copy-start.1
  26.1 16.9 %project.4 = (f32[80,512]{1,0:T(8,128)}, f32[80,512]{1,0:T(8,128)}, f32[80,512]{1,0:T(8,128)}) custom-call(s32[1]{0:T(128)} %bitcast.1.refs_0_, s32[8,128]{1,0:T(8,128)} %refs_1_.5, s32[8,128]{1,0:T(8,128)} %refs_2_.5, bf16[80,65536]{1,0:T(8,128)(2,1)} %get-tuple-element.19.refs_3_), custom_call_target="tpu_custom_call" | custom-call | flops 32212254720 | bytes 10485760 | tf_op jit(solution)/shard_map/project/pallas_call | solution.py:158
  43.1 1.6 %collective-permute-start.4 = (f32[80,512]{1,0:T(8,128)}, f32[80,512]{1,0:T(8,128)S(1)}, u32[]{:S(2)}, u32[]{:S(2)}) collective-permute-start(f32[80,512]{1,0:T(8,128)} %get-tuple-element.20), channel_id=1, source_target_pairs={{0,64},{16,80},{32,96},{48,112},{64,128},{80,144},{96,160},{112,17... | collective-permute-start | bytes 491528 | tf_op jit(solution)/shard_map/ppermute | solution.py:239
  44.7 2.9 %collective-permute-start.5 = (f32[80,512]{1,0:T(8,128)}, f32[80,512]{1,0:T(8,128)S(1)}, u32[]{:S(2)}, u32[]{:S(2)}) collective-permute-start(f32[80,512]{1,0:T(8,128)} %get-tuple-element.21), channel_id=1, source_target_pairs={{0,48},{16,64},{32,80},{48,96},{64,112},{80,128},{96,144},{112,160... | collective-permute-start | bytes 491528 | tf_op jit(solution)/shard_map/ppermute | solution.py:239
  47.7 2.6 %collective-permute-start.6 = (f32[80,512]{1,0:T(8,128)}, f32[80,512]{1,0:T(8,128)S(1)}, u32[]{:S(2)}, u32[]{:S(2)}) collective-permute-start(f32[80,512]{1,0:T(8,128)} %get-tuple-element.22), channel_id=1, source_target_pairs={{0,240},{16,0},{32,16},{48,32},{64,48},{80,64},{96,80},{112,96},{1... | collective-permute-start | bytes 491528 | tf_op jit(solution)/shard_map/ppermute | solution.py:239
  50.2 0.0 copy-done.4
  50.2 4.5 %collective-permute-start = (f32[80,512]{1,0:T(8,128)S(1)}, f32[80,512]{1,0:T(8,128)S(1)}, u32[]{:S(2)}, u32[]{:S(2)}) collective-permute-start(f32[80,512]{1,0:T(8,128)S(1)} %copy-done.4), channel_id=1, source_target_pairs={{0,128},{16,144},{32,160},{48,176},{64,192},{80,208},{96,224},{112... | collective-permute-start | bytes 491528 | tf_op jit(solution)/shard_map/ppermute | solution.py:239
  54.7 0.0 copy-done.3
  54.7 0.0 collective-permute-start.1
  54.7 1.4 %collective-permute-done.4.refs_4_ = f32[80,512]{1,0:T(8,128)S(1)} collective-permute-done((f32[80,512]{1,0:T(8,128)}, f32[80,512]{1,0:T(8,128)S(1)}, u32[]{:S(2)}, u32[]{:S(2)}) %collective-permute-start.4) | collective-permute-done | bytes 163872 | tf_op jit(solution)/shard_map/ppermute | solution.py:239
  56.1 0.0 copy-done.2
  56.1 3.2 %collective-permute-start.2 = (f32[80,512]{1,0:T(8,128)S(1)}, f32[80,512]{1,0:T(8,128)S(1)}, u32[]{:S(2)}, u32[]{:S(2)}) collective-permute-start(f32[80,512]{1,0:T(8,128)S(1)} %copy-done.2), channel_id=1, source_target_pairs={{0,192},{16,208},{32,224},{48,240},{64,0},{80,16},{96,32},{112,48}... | collective-permute-start | bytes 491528 | tf_op jit(solution)/shard_map/ppermute | solution.py:239
  59.3 1.5 %collective-permute-done.5.refs_5_ = f32[80,512]{1,0:T(8,128)S(1)} collective-permute-done((f32[80,512]{1,0:T(8,128)}, f32[80,512]{1,0:T(8,128)S(1)}, u32[]{:S(2)}, u32[]{:S(2)}) %collective-permute-start.5) | collective-permute-done | bytes 163872 | tf_op jit(solution)/shard_map/ppermute | solution.py:239
  60.9 0.0 copy-done.1
  60.9 11.2 %collective-permute-start.3 = (f32[80,512]{1,0:T(8,128)S(1)}, f32[80,512]{1,0:T(8,128)S(1)}, u32[]{:S(2)}, u32[]{:S(2)}) collective-permute-start(f32[80,512]{1,0:T(8,128)S(1)} %copy-done.1), channel_id=1, source_target_pairs={{0,176},{16,192},{32,208},{48,224},{64,240},{80,0},{96,16},{112,32... | collective-permute-start | bytes 491528 | tf_op jit(solution)/shard_map/ppermute | solution.py:239
  72.1 8.9 %project.5.refs_7_ = f32[80,512]{1,0:T(8,128)} custom-call(s32[1]{0:T(128)} %bitcast.1.refs_0_, s32[8,128]{1,0:T(8,128)} %refs_1_.5, s32[8,128]{1,0:T(8,128)} %refs_2_.5, bf16[80,65536]{1,0:T(8,128)(2,1)} %get-tuple-element.19.refs_3_), custom_call_target="tpu_custom_call" | custom-call | flops 10737418240 | bytes 10485760 | tf_op jit(solution)/shard_map/project/pallas_call | solution.py:158
  81.0 0.0 collective-permute-done.6.refs_6_
  81.0 0.0 collective-permute-done.refs_0_
  81.0 0.0 collective-permute-done.1.refs_1_
  81.0 0.0 collective-permute-done.2.refs_2_
  81.0 0.7 collective-permute-done.3.refs_3_
  81.7 0.0 copy-start
  81.7 0.9 copy-done
  82.6 0.1 merge.1
  82.7 15.6 %all_to_all.10.own_ref = f32[8,16,512]{2,1,0:T(8,128)S(1)} all-to-all(f32[8,16,512]{2,1,0:T(8,128)S(1)} %get-tuple-element.24), channel_id=1, replica_groups={{0,2,4,6,8,10,12,14},{1,3,5,7,9,11,13,15},{16,18,20,22,24,26,28,30},{17..., dimensions={0} | all-to-all | bytes 524288 | tf_op jit(solution)/shard_map/all_to_all | solution.py:264
  98.3 0.0 collective-permute-start.7
  98.3 1.5 %collective-permute-done.7.other_ref = f32[8,16,512]{2,1,0:T(8,128)S(1)} collective-permute-done((f32[8,16,512]{2,1,0:T(8,128)S(1)}, f32[8,16,512]{2,1,0:T(8,128)S(1)}, u32[]{:S(2)}, u32[]{:S(2)}) %collective-permute-start.7) | collective-permute-done | bytes 262176 | tf_op jit(solution)/shard_map/ppermute | solution.py:267
  99.9 0.6 dots.1
  100.5 16.9 %all_to_all.11.parts_ref = f32[16,24,128]{2,1,0:T(8,128)S(1)} all-to-all(f32[16,24,128]{2,1,0:T(8,128)S(1)} %bitcast.5), channel_id=1, replica_groups=mesh['feat'=16,'cand'=16] {'feat'}, dimensions={0} | all-to-all | bytes 393216 | tf_op jit(solution)/shard_map/all_to_all | solution.py:277
  117.4 0.7 score.1
Async XLA Ops:
  26.1 24.1 %copy-start.4 = (f32[80,512]{1,0:T(8,128)S(1)}, f32[80,512]{1,0:T(8,128)}, u32[]{:S(2)}) copy-start(f32[80,512]{1,0:T(8,128)} %get-tuple-element.15) | copy-start | bytes 491524
  26.1 28.6 %copy-start.3 = (f32[80,512]{1,0:T(8,128)S(1)}, f32[80,512]{1,0:T(8,128)}, u32[]{:S(2)}) copy-start(f32[80,512]{1,0:T(8,128)} %get-tuple-element.16) | copy-start | bytes 491524
  26.1 30.0 %copy-start.2 = (f32[80,512]{1,0:T(8,128)S(1)}, f32[80,512]{1,0:T(8,128)}, u32[]{:S(2)}) copy-start(f32[80,512]{1,0:T(8,128)} %get-tuple-element.17) | copy-start | bytes 491524
  26.1 34.8 %copy-start.1 = (f32[80,512]{1,0:T(8,128)S(1)}, f32[80,512]{1,0:T(8,128)}, u32[]{:S(2)}) copy-start(f32[80,512]{1,0:T(8,128)} %get-tuple-element.18) | copy-start | bytes 491524
  43.1 13.0 %collective-permute-start.4 = (f32[80,512]{1,0:T(8,128)}, f32[80,512]{1,0:T(8,128)S(1)}, u32[]{:S(2)}, u32[]{:S(2)}) collective-permute-start(f32[80,512]{1,0:T(8,128)} %get-tuple-element.20), channel_id=1, source_target_pairs={{0,64},{16,80},{32,96},{48,112},{64,128},{80,144},{96,160},{112,17... | collective-permute-start | bytes 491528 | tf_op jit(solution)/shard_map/ppermute | solution.py:239
  44.7 16.2 %collective-permute-start.5 = (f32[80,512]{1,0:T(8,128)}, f32[80,512]{1,0:T(8,128)S(1)}, u32[]{:S(2)}, u32[]{:S(2)}) collective-permute-start(f32[80,512]{1,0:T(8,128)} %get-tuple-element.21), channel_id=1, source_target_pairs={{0,48},{16,64},{32,80},{48,96},{64,112},{80,128},{96,144},{112,160... | collective-permute-start | bytes 491528 | tf_op jit(solution)/shard_map/ppermute | solution.py:239
  47.7 33.3 %collective-permute-start.6 = (f32[80,512]{1,0:T(8,128)}, f32[80,512]{1,0:T(8,128)S(1)}, u32[]{:S(2)}, u32[]{:S(2)}) collective-permute-start(f32[80,512]{1,0:T(8,128)} %get-tuple-element.22), channel_id=1, source_target_pairs={{0,240},{16,0},{32,16},{48,32},{64,48},{80,64},{96,80},{112,96},{1... | collective-permute-start | bytes 491528 | tf_op jit(solution)/shard_map/ppermute | solution.py:239
  50.2 30.8 %collective-permute-start = (f32[80,512]{1,0:T(8,128)S(1)}, f32[80,512]{1,0:T(8,128)S(1)}, u32[]{:S(2)}, u32[]{:S(2)}) collective-permute-start(f32[80,512]{1,0:T(8,128)S(1)} %copy-done.4), channel_id=1, source_target_pairs={{0,128},{16,144},{32,160},{48,176},{64,192},{80,208},{96,224},{112... | collective-permute-start | bytes 491528 | tf_op jit(solution)/shard_map/ppermute | solution.py:239
  54.7 26.3 %collective-permute-start.1 = (f32[80,512]{1,0:T(8,128)S(1)}, f32[80,512]{1,0:T(8,128)S(1)}, u32[]{:S(2)}, u32[]{:S(2)}) collective-permute-start(f32[80,512]{1,0:T(8,128)S(1)} %copy-done.3), channel_id=1, source_target_pairs={{0,112},{16,128},{32,144},{48,160},{64,176},{80,192},{96,208},{112... | collective-permute-start | bytes 491528 | tf_op jit(solution)/shard_map/ppermute | solution.py:239
  56.1 24.9 %collective-permute-start.2 = (f32[80,512]{1,0:T(8,128)S(1)}, f32[80,512]{1,0:T(8,128)S(1)}, u32[]{:S(2)}, u32[]{:S(2)}) collective-permute-start(f32[80,512]{1,0:T(8,128)S(1)} %copy-done.2), channel_id=1, source_target_pairs={{0,192},{16,208},{32,224},{48,240},{64,0},{80,16},{96,32},{112,48}... | collective-permute-start | bytes 491528 | tf_op jit(solution)/shard_map/ppermute | solution.py:239
  60.9 20.8 %collective-permute-start.3 = (f32[80,512]{1,0:T(8,128)S(1)}, f32[80,512]{1,0:T(8,128)S(1)}, u32[]{:S(2)}, u32[]{:S(2)}) collective-permute-start(f32[80,512]{1,0:T(8,128)S(1)} %copy-done.1), channel_id=1, source_target_pairs={{0,176},{16,192},{32,208},{48,224},{64,240},{80,0},{96,16},{112,32... | collective-permute-start | bytes 491528 | tf_op jit(solution)/shard_map/ppermute | solution.py:239
  81.7 0.9 copy-start
  98.3 1.5 %collective-permute-start.7 = (f32[8,16,512]{2,1,0:T(8,128)S(1)}, f32[8,16,512]{2,1,0:T(8,128)S(1)}, u32[]{:S(2)}, u32[]{:S(2)}) collective-permute-start(f32[8,16,512]{2,1,0:T(8,128)S(1)} %all_to_all.10.own_ref), channel_id=1, source_target_pairs={{0,1},{1,0},{2,3},{3,2},{4,5},{5,4},{6,7},{7,6},{8,9},{9,8},{10,11... | collective-permute-start | bytes 786440 | tf_op jit(solution)/shard_map/ppermute | solution.py:267

commit v3 on v2

--- a/solution.py
+++ b/solution.py
@@ -13,9 +13,9 @@
 FB = 64
 SLOTS = 8
 VPT = 4
-GRANT = 62 << 20
+GRANT = 32 << 20
+SMALL_GRANT = 16 << 20
 AHEAD = 2
-ORDER = ((4, 5, 2, 3), (6, 7, 1), (0,))
 
 
 def wrap32(value):
@@ -40,19 +40,15 @@
 
 def project(slots, adam, devices, me_ref, blocks_ref, seeds_ref, *refs):
     if adam:
-        cand_hbm, val_hbm, moment_hbm, *out_refs = refs
-        *out_refs, rows_hbm, rows_ref, acc_ref, table_ref, sem, cand_ref, moment_ref = out_refs
+        cand_hbm, val_hbm, moment_hbm, out_ref, rows_ref, acc_ref, table_ref, cand_ref, moment_ref, sem = refs
     else:
-        rows_hbm, *out_refs = refs
-        *out_refs, rows_ref, acc_ref, table_ref, sem = out_refs
+        rows_ref, out_ref, acc_ref, table_ref = refs
     count = len(slots)
     height, length = rows_ref.shape
     blocks = length // PB
 
     def copies(block):
         at = pl.ds(pl.multiple_of(block * PB, PB), PB)
-        if not adam:
-            return (pltpu.make_async_copy(rows_hbm.at[:, at], rows_ref.at[:, at], sem.at[0, block]),)
         ncand = cand_ref.shape[0]
         return (
             pltpu.make_async_copy(moment_hbm.at[:, at], moment_ref.at[:, at], sem.at[0, block]),
@@ -60,13 +56,10 @@
             pltpu.make_async_copy(val_hbm.at[:, at], rows_ref.at[ncand:, at], sem.at[2, block]),
         )
 
-    def copy_out(block):
-        at = pl.ds(pl.multiple_of(block * PB, PB), PB)
-        return pltpu.make_async_copy(rows_ref.at[:, at], rows_hbm.at[:, at], sem.at[3, block])
-
-    for block in range(AHEAD):
-        for copy in copies(block):
-            copy.start()
+    if adam:
+        for block in range(AHEAD):
+            for copy in copies(block):
+                copy.start()
     me = me_ref[0]
     for n, slot in enumerate(slots):
         owner = lax.rem(me + devices - offset_of(slot, devices // SLOTS), devices)
@@ -80,20 +73,19 @@
 
     def one_block(block, carry):
         at = pl.ds(pl.multiple_of(block * PB, PB), PB)
-
-        @pl.when(block + AHEAD < blocks)
-        def _():
-            for copy in copies(block + AHEAD):
-                copy.start()
-
-        for copy in copies(block):
-            copy.wait()
         if adam:
+
+            @pl.when(block + AHEAD < blocks)
+            def _():
+                for copy in copies(block + AHEAD):
+                    copy.start()
+
+            for copy in copies(block):
+                copy.wait()
             wide = cand_ref[:, at].astype(jnp.float32)
             square = 0.999 * moment_ref[:, at] + (0.001 * wide) * wide
             den = square * lax.rsqrt(square) + 1e-08
             rows_ref[: cand_ref.shape[0], at] = (wide * lax.rsqrt(den * den)).astype(jnp.bfloat16)
-            copy_out(block).start()
         mixed = []
         for n in range(count):
             mixed.append(column ^ fold(table_ref[0, n, block]))
@@ -121,10 +113,7 @@
     lax.fori_loop(0, blocks, one_block, 0)
     for n in range(count):
         for pair in range(acc_ref.shape[1]):
-            out_refs[n][:, pair * 2 * FB : (pair + 1) * 2 * FB] = acc_ref[n, pair]
-    if adam:
-        for block in range(blocks):
-            copy_out(block).wait()
+            out_ref[n, :, pair * 2 * FB : (pair + 1) * 2 * FB] = acc_ref[n, pair]
 
 
 def projected(slots, tables, operands, adam, devices):
@@ -140,28 +129,27 @@
         height, length = rows.shape
     blocks = length // PB
     width = blocks * FB
-    out_shape = [jax.ShapeDtypeStruct((height, width), jnp.float32)] * count
-    out_specs = [vmem] * count
+    out_shape = [jax.ShapeDtypeStruct((count, height, width), jnp.float32)]
+    out_specs = [vmem]
     scratch = [
-        pltpu.VMEM((height, length), jnp.bfloat16),
         pltpu.VMEM((count, width // (2 * FB), height, 2 * FB), jnp.float32),
         pltpu.SMEM((2, count, blocks), jnp.int32),
-        pltpu.SemaphoreType.DMA((4, blocks)),
     ]
     if adam:
         out_shape.append(jax.ShapeDtypeStruct((height, length), jnp.bfloat16))
-        out_specs.append(pl.BlockSpec(memory_space=pl.ANY))
+        out_specs.append(vmem)
         scratch += [
             pltpu.VMEM(cand.shape, jnp.bfloat16),
             pltpu.VMEM(moment.shape, jnp.float32),
+            pltpu.SemaphoreType.DMA((3, blocks)),
         ]
     return pl.pallas_call(
         lambda *refs: project(slots, adam, devices, *refs),
         out_shape=out_shape,
-        in_specs=[smem, smem, smem] + [pl.BlockSpec(memory_space=pl.ANY)] * len(operands),
+        in_specs=[smem, smem, smem] + [pl.BlockSpec(memory_space=pltpu.HBM) if adam else vmem] * len(operands),
         out_specs=out_specs,
         scratch_shapes=scratch,
-        compiler_params=pltpu.CompilerParams(vmem_limit_bytes=GRANT),
+        compiler_params=pltpu.CompilerParams(vmem_limit_bytes=GRANT if adam else SMALL_GRANT),
         cost_estimate=pl.CostEstimate(
             flops=2 * count * width * height * PB * 16,
             bytes_accessed=2 * height * length,
@@ -171,11 +159,13 @@
     )(*tables, *operands)
 
 
-def merge_kernel(*refs):
-    *term_refs, cand_ref, val_ref = refs
-    total = term_refs[0][...]
-    for term_ref in term_refs[1:]:
-        total = total + term_ref[...]
+def join_kernel(odd_ref, even_ref, *out_refs):
+    for n, out_ref in enumerate(out_refs):
+        out_ref[...] = odd_ref[n + 1] + even_ref[n]
+
+
+def merge_kernel(odd_ref, kept_ref, first_ref, second_ref, third_ref, cand_ref, val_ref):
+    total = (odd_ref[0] + kept_ref[0]) + (first_ref[...] + second_ref[...]) + third_ref[...]
     total = total * (1.0 / math.sqrt(SLOTS * PB))
     ncand = cand_ref.shape[0]
     cand_ref[...] = total[:ncand]
@@ -231,26 +221,34 @@
     ncand = cand_grads.shape[0]
     nval = val_grads.shape[0]
 
+    cand_grads, val_grads, second_moment, slot_blocks, slot_seeds = (
+        pltpu.with_memory_space_constraint(x, pltpu.HBM)
+        for x in (cand_grads, val_grads, second_moment[None, :], slot_blocks, slot_seeds)
+    )
     tables = (lax.axis_index("feat").reshape(1), slot_blocks, slot_seeds)
 
-    def send(part, slot):
-        offset = offset_of(slot, devices // SLOTS)
-        pairs = [(j, (j - offset) % devices) for j in range(devices)]
-        return lax.ppermute(part, "feat", pairs)
-
-    rows = None
-    terms = []
-    for slots in ORDER:
-        if rows is None:
-            operands = (cand_grads, val_grads, second_moment[None, :])
-            *parts, rows = projected(slots, tables, operands, True, devices)
-        else:
-            parts = projected(slots, tables, (rows,), False, devices)
-        for part, slot in zip(parts, slots):
-            terms.append(send(part, slot) if slot else part)
+    def back(part, steps):
+        return lax.ppermute(part, "feat", [(j, (j - steps) % devices) for j in range(devices)])
+
+    apart = devices // (SLOTS // 2)
     small = pltpu.CompilerParams(vmem_limit_bytes=8 << 20)
+    operands = (cand_grads, val_grads, second_moment)
+    odd, rows = projected((1, 3, 5, 7), tables, operands, True, devices)
+    odd = back(odd, 1)
+    (even,) = projected((2, 4, 6), tables, (rows,), False, devices)
+    joined = pl.pallas_call(
+        join_kernel,
+        out_shape=[jax.ShapeDtypeStruct(even.shape[1:], jnp.float32)] * 3,
+        compiler_params=small,
+        name="join",
+    )(odd, even)
+    second = back(joined[1], 2 * apart)
+    first = back(joined[0], apart)
+    third = back(joined[2], 3 * apart)
+    (kept,) = projected((0,), tables, (rows,), False, devices)
+
     pairs = groups // 2
-    width = terms[0].shape[1]
+    width = first.shape[1]
     cand_part, val_part = pl.pallas_call(
         merge_kernel,
         out_shape=[
@@ -259,7 +257,7 @@
         ],
         compiler_params=small,
         name="merge",
-    )(*terms)
+    )(odd, kept, first, second, third)
     same_core = [[2 * m + core for m in range(pairs)] for core in range(2)]
     val_own = lax.all_to_all(
         val_part, "cand", 0, 0, tiled=True, axis_index_groups=same_core

time: 119 us -> 99.5 us (0.84)
  starting transfers between devices: 26.1 us -> 10.5 us
  Pallas kernels: 53.3 us -> 47 us
  waiting for transfers between devices: 5.17 us -> 8.95 us
    ppermute x7 -> x4, starting transfers between devices: 26.1 us -> 10.5 us  [back(): lax.ppermute(part, 'feat', [(j, (j - steps) % devices) for j in range(dev...]
    pallas_call x3, Pallas kernels: 51.9 us -> 45.5 us  [projected(): pl.pallas_call(lambda *refs: project(slots, adam, devices, *refs), out_sh...]
    ppermute x7 -> x4, waiting for transfers between devices: 3.63 us -> 7.42 us  [back(): lax.ppermute(part, 'feat', [(j, (j - steps) % devices) for j in range(dev...]
  transfers between devices with their start and end apart: 8 -> 5, of which waited for: 4 -> 3; matrix products, arithmetic and copies ran while one was open for 0% -> 0% of each run, Pallas kernels for 8% -> 22%
where the time goes in v3:
time: 99.5 us; the launch traced here: 98.1 us
  Pallas kernels  47 us (47%)
  blocking collectives  31.7 us (32%)
  starting transfers between devices  10.5 us (11%)
  waiting for transfers between devices  8.95 us (9%)
    pallas_call x3, Pallas kernels, projected(): pl.pallas_call(lambda *refs: project(slots, adam, devices, *refs), out_sh...  45.5 us
    all_to_all x1, blocking collectives, body(): parts = lax.all_to_all(packed, 'feat', 0, 0, tiled=True)  17 us
    all_to_all x1, blocking collectives, body(): lax.all_to_all(val_part, 'cand', 0, 0, tiled=True, axis_index_groups=same...  14.7 us
    ppermute x4, starting transfers between devices, back(): lax.ppermute(part, 'feat', [(j, (j - steps) % devices) for j in range(dev...  10.5 us
    ppermute x4, waiting for transfers between devices, back(): lax.ppermute(part, 'feat', [(j, (j - steps) % devices) for j in range(dev...  7.42 us
  transfers between devices with their start and end apart: 5, of which 3 were waited for; matrix products, arithmetic and copies ran while one was open for 0% of the time, Pallas kernels for 22%

profile of v3, /device:TPU:0, one launch (start us, length us, event | category | flops | bytes accessed | tf_op | source)
XLA Modules:
  0.0 98.1 jit_solution(13885847916015068207)
XLA Ops:
  0.0 24.4 %project.3 = (f32[4,80,512]{2,1,0:T(8,128)S(1)}, bf16[80,65536]{1,0:T(8,128)(2,1)S(1)}) custom-call(s32[1]{0:T(128)} %bitcast.1.refs_0_, s32[8,128]{1,0:T(8,128)} %refs_1_.5, s32[8,128]{1,0:T(8,128)} %refs_2_.5, bf16[64,65536]{1,0:T(8,128)(2,1)} %refs_3_.1, bf16[16,65536]{1,0:T(8,128)(2,1)} %refs_4_.1, f32[1,65536]{1,0:T(1,128)} %bitcast.6), custom_call_target="tpu_custom_call" | custom-call | flops 42949672960 | bytes 10485760 | tf_op jit(solution)/shard_map/project/pallas_call | solution.py:146
  24.4 5.2 %collective-permute-start = (f32[4,80,512]{2,1,0:T(8,128)S(1)}, f32[4,80,512]{2,1,0:T(8,128)S(1)}, u32[]{:S(2)}, u32[]{:S(2)}) collective-permute-start(f32[4,80,512]{2,1,0:T(8,128)S(1)} %get-tuple-element.12), channel_id=1, source_target_pairs={{0,240},{16,0},{32,16},{48,32},{64,48},{80,64},{96,80},{112,96},{1... | collective-permute-start | bytes 1966088 | tf_op jit(solution)/shard_map/ppermute | solution.py:231
  29.6 14.6 %project.5.even_ref = f32[3,80,512]{2,1,0:T(8,128)S(1)} custom-call(s32[1]{0:T(128)} %bitcast.1.refs_0_, s32[8,128]{1,0:T(8,128)} %refs_1_.5, s32[8,128]{1,0:T(8,128)} %refs_2_.5, bf16[80,65536]{1,0:T(8,128)(2,1)S(1)} %get-tuple-element.13.refs_3_), custom_call_target="tpu_custom_call" | custom-call | flops 32212254720 | bytes 10485760 | tf_op jit(solution)/shard_map/project/pallas_call | solution.py:146
  44.2 0.0 collective-permute-done.odd_ref
  44.2 0.1 join.1
  44.3 1.5 %collective-permute-start.1 = (f32[80,512]{1,0:T(8,128)S(1)}, f32[80,512]{1,0:T(8,128)S(1)}, u32[]{:S(2)}, u32[]{:S(2)}) collective-permute-start(f32[80,512]{1,0:T(8,128)S(1)} %get-tuple-element.14), channel_id=1, source_target_pairs={{0,192},{16,208},{32,224},{48,240},{64,0},{80,16},{96,32},{112,48}... | collective-permute-start | bytes 491528 | tf_op jit(solution)/shard_map/ppermute | solution.py:231
  45.8 0.9 collective-permute-start.2
  46.7 2.8 %collective-permute-start.3 = (f32[80,512]{1,0:T(8,128)S(1)}, f32[80,512]{1,0:T(8,128)S(1)}, u32[]{:S(2)}, u32[]{:S(2)}) collective-permute-start(f32[80,512]{1,0:T(8,128)S(1)} %get-tuple-element.16), channel_id=1, source_target_pairs={{0,64},{16,80},{32,96},{48,112},{64,128},{80,144},{96,160},{112,17... | collective-permute-start | bytes 491528 | tf_op jit(solution)/shard_map/ppermute | solution.py:231
  49.5 6.6 %project.4.kept_ref = f32[1,80,512]{2,1,0:T(8,128)S(1)} custom-call(s32[1]{0:T(128)} %bitcast.1.refs_0_, s32[8,128]{1,0:T(8,128)} %refs_1_.5, s32[8,128]{1,0:T(8,128)} %refs_2_.5, bf16[80,65536]{1,0:T(8,128)(2,1)S(1)} %get-tuple-element.13.refs_3_), custom_call_target="tpu_custom_call" | custom-call | flops 10737418240 | bytes 10485760 | tf_op jit(solution)/shard_map/project/pallas_call | solution.py:146
  56.1 0.0 collective-permute-done.1.first_ref
  56.1 5.9 %collective-permute-done.2.second_ref = f32[80,512]{1,0:T(8,128)S(1)} collective-permute-done((f32[80,512]{1,0:T(8,128)S(1)}, f32[80,512]{1,0:T(8,128)S(1)}, u32[]{:S(2)}, u32[]{:S(2)}) %collective-permute-start.2) | collective-permute-done | bytes 163872 | tf_op jit(solution)/shard_map/ppermute | solution.py:231
  62.0 1.5 %collective-permute-done.3.third_ref = f32[80,512]{1,0:T(8,128)S(1)} collective-permute-done((f32[80,512]{1,0:T(8,128)S(1)}, f32[80,512]{1,0:T(8,128)S(1)}, u32[]{:S(2)}, u32[]{:S(2)}) %collective-permute-start.3) | collective-permute-done | bytes 163872 | tf_op jit(solution)/shard_map/ppermute | solution.py:231
  63.5 0.1 merge.1
  63.6 14.7 %all_to_all.10.own_ref = f32[8,16,512]{2,1,0:T(8,128)S(1)} all-to-all(f32[8,16,512]{2,1,0:T(8,128)S(1)} %get-tuple-element.18), channel_id=1, replica_groups={{0,2,4,6,8,10,12,14},{1,3,5,7,9,11,13,15},{16,18,20,22,24,26,28,30},{17..., dimensions={0} | all-to-all | bytes 524288 | tf_op jit(solution)/shard_map/all_to_all | solution.py:262
  78.2 0.0 collective-permute-start.4
  78.3 1.5 %collective-permute-done.4.other_ref = f32[8,16,512]{2,1,0:T(8,128)S(1)} collective-permute-done((f32[8,16,512]{2,1,0:T(8,128)S(1)}, f32[8,16,512]{2,1,0:T(8,128)S(1)}, u32[]{:S(2)}, u32[]{:S(2)}) %collective-permute-start.4) | collective-permute-done | bytes 262176 | tf_op jit(solution)/shard_map/ppermute | solution.py:265
  79.8 0.6 dots.1
  80.4 17.0 %all_to_all.11.parts_ref = f32[16,24,128]{2,1,0:T(8,128)S(1)} all-to-all(f32[16,24,128]{2,1,0:T(8,128)S(1)} %bitcast.5), channel_id=1, replica_groups=mesh['feat'=16,'cand'=16] {'feat'}, dimensions={0} | all-to-all | bytes 393216 | tf_op jit(solution)/shard_map/all_to_all | solution.py:275
  97.4 0.7 score.1
Async XLA Ops:
  24.4 19.8 %collective-permute-start = (f32[4,80,512]{2,1,0:T(8,128)S(1)}, f32[4,80,512]{2,1,0:T(8,128)S(1)}, u32[]{:S(2)}, u32[]{:S(2)}) collective-permute-start(f32[4,80,512]{2,1,0:T(8,128)S(1)} %get-tuple-element.12), channel_id=1, source_target_pairs={{0,240},{16,0},{32,16},{48,32},{64,48},{80,64},{96,80},{112,96},{1... | collective-permute-start | bytes 1966088 | tf_op jit(solution)/shard_map/ppermute | solution.py:231
  44.3 11.8 %collective-permute-start.1 = (f32[80,512]{1,0:T(8,128)S(1)}, f32[80,512]{1,0:T(8,128)S(1)}, u32[]{:S(2)}, u32[]{:S(2)}) collective-permute-start(f32[80,512]{1,0:T(8,128)S(1)} %get-tuple-element.14), channel_id=1, source_target_pairs={{0,192},{16,208},{32,224},{48,240},{64,0},{80,16},{96,32},{112,48}... | collective-permute-start | bytes 491528 | tf_op jit(solution)/shard_map/ppermute | solution.py:231
  45.8 16.2 %collective-permute-start.2 = (f32[80,512]{1,0:T(8,128)S(1)}, f32[80,512]{1,0:T(8,128)S(1)}, u32[]{:S(2)}, u32[]{:S(2)}) collective-permute-start(f32[80,512]{1,0:T(8,128)S(1)} %get-tuple-element.15), channel_id=1, source_target_pairs={{0,128},{16,144},{32,160},{48,176},{64,192},{80,208},{96,224},{112... | collective-permute-start | bytes 491528 | tf_op jit(solution)/shard_map/ppermute | solution.py:231
  46.7 16.8 %collective-permute-start.3 = (f32[80,512]{1,0:T(8,128)S(1)}, f32[80,512]{1,0:T(8,128)S(1)}, u32[]{:S(2)}, u32[]{:S(2)}) collective-permute-start(f32[80,512]{1,0:T(8,128)S(1)} %get-tuple-element.16), channel_id=1, source_target_pairs={{0,64},{16,80},{32,96},{48,112},{64,128},{80,144},{96,160},{112,17... | collective-permute-start | bytes 491528 | tf_op jit(solution)/shard_map/ppermute | solution.py:231
  78.2 1.5 %collective-permute-start.4 = (f32[8,16,512]{2,1,0:T(8,128)S(1)}, f32[8,16,512]{2,1,0:T(8,128)S(1)}, u32[]{:S(2)}, u32[]{:S(2)}) collective-permute-start(f32[8,16,512]{2,1,0:T(8,128)S(1)} %all_to_all.10.own_ref), channel_id=1, source_target_pairs={{0,1},{1,0},{2,3},{3,2},{4,5},{5,4},{6,7},{7,6},{8,9},{9,8},{10,11... | collective-permute-start | bytes 786440 | tf_op jit(solution)/shard_map/ppermute | solution.py:265

commit v4 on v3

--- a/solution.py
+++ b/solution.py
@@ -161,11 +161,14 @@
 
 def join_kernel(odd_ref, even_ref, *out_refs):
     for n, out_ref in enumerate(out_refs):
-        out_ref[...] = odd_ref[n + 1] + even_ref[n]
-
-
-def merge_kernel(odd_ref, kept_ref, first_ref, second_ref, third_ref, cand_ref, val_ref):
-    total = (odd_ref[0] + kept_ref[0]) + (first_ref[...] + second_ref[...]) + third_ref[...]
+        out_ref[...] = odd_ref[n] + even_ref[n]
+
+
+def merge_kernel(*refs):
+    *term_refs, cand_ref, val_ref = refs
+    total = term_refs[0][...]
+    for term_ref in term_refs[1:]:
+        total = total + term_ref[...]
     total = total * (1.0 / math.sqrt(SLOTS * PB))
     ncand = cand_ref.shape[0]
     cand_ref[...] = total[:ncand]
@@ -233,7 +236,7 @@
     apart = devices // (SLOTS // 2)
     small = pltpu.CompilerParams(vmem_limit_bytes=8 << 20)
     operands = (cand_grads, val_grads, second_moment)
-    odd, rows = projected((1, 3, 5, 7), tables, operands, True, devices)
+    odd, rows = projected((3, 5, 7), tables, operands, True, devices)
     odd = back(odd, 1)
     (even,) = projected((2, 4, 6), tables, (rows,), False, devices)
     joined = pl.pallas_call(
@@ -245,7 +248,10 @@
     second = back(joined[1], 2 * apart)
     first = back(joined[0], apart)
     third = back(joined[2], 3 * apart)
+    (beside,) = projected((1,), tables, (rows,), False, devices)
+    beside = back(beside[0], 1)
     (kept,) = projected((0,), tables, (rows,), False, devices)
+    kept = kept[0]
 
     pairs = groups // 2
     width = first.shape[1]
@@ -257,7 +263,7 @@
         ],
         compiler_params=small,
         name="merge",
-    )(odd, kept, first, second, third)
+    )(beside, kept, first, second, third)
     same_core = [[2 * m + core for m in range(pairs)] for core in range(2)]
     val_own = lax.all_to_all(
         val_part, "cand", 0, 0, tiled=True, axis_index_groups=same_core

time: 99.5 us -> 103 us (1.035)
  Pallas kernels: 47 us -> 50 us
    pallas_call x3 -> x4, Pallas kernels: 45.5 us -> 48.5 us  [projected(): pl.pallas_call(lambda *refs: project(slots, adam, devices, *refs), out_sh...]
    ppermute x4 -> x5, waiting for transfers between devices: 7.42 us -> 7.43 us  [back(): lax.ppermute(part, 'feat', [(j, (j - steps) % devices) for j in range(dev...]
    ppermute x4 -> x5, starting transfers between devices: 10.5 us -> 10.5 us  [back(): lax.ppermute(part, 'feat', [(j, (j - steps) % devices) for j in range(dev...]
  transfers between devices with their start and end apart: 5 -> 6, of which waited for: 3 -> 4; matrix products, arithmetic and copies ran while one was open for 0% -> 0% of each run, Pallas kernels for 22% -> 21%
where the time goes in v4:
time: 103 us; the launch traced here: 101 us
  Pallas kernels  50 us (49%)
  blocking collectives  31.6 us (31%)
  starting transfers between devices  10.5 us (10%)
  waiting for transfers between devices  8.96 us (9%)
    pallas_call x4, Pallas kernels, projected(): pl.pallas_call(lambda *refs: project(slots, adam, devices, *refs), out_sh...  48.5 us
    all_to_all x1, blocking collectives, body(): parts = lax.all_to_all(packed, 'feat', 0, 0, tiled=True)  16.3 us
    all_to_all x1, blocking collectives, body(): lax.all_to_all(val_part, 'cand', 0, 0, tiled=True, axis_index_groups=same...  15.4 us
    ppermute x5, starting transfers between devices, back(): lax.ppermute(part, 'feat', [(j, (j - steps) % devices) for j in range(dev...  10.5 us
    ppermute x5, waiting for transfers between devices, back(): lax.ppermute(part, 'feat', [(j, (j - steps) % devices) for j in range(dev...  7.43 us
  transfers between devices with their start and end apart: 6, of which 4 were waited for; matrix products, arithmetic and copies ran while one was open for 0% of the time, Pallas kernels for 21%

profile of v4, /device:TPU:0, one launch (start us, length us, event | category | flops | bytes accessed | tf_op | source)
XLA Modules:
  0.0 101.1 jit_solution(1944049934058391250)
XLA Ops:
  0.0 20.8 %project.4 = (f32[3,80,512]{2,1,0:T(8,128)S(1)}, bf16[80,65536]{1,0:T(8,128)(2,1)S(1)}) custom-call(s32[1]{0:T(128)} %bitcast.1.refs_0_, s32[8,128]{1,0:T(8,128)} %refs_1_.7, s32[8,128]{1,0:T(8,128)} %refs_2_.7, bf16[64,65536]{1,0:T(8,128)(2,1)} %refs_3_.1, bf16[16,65536]{1,0:T(8,128)(2,1)} %refs_4_.1, f32[1,65536]{1,0:T(1,128)} %bitcast.10), custom_call_target="tpu_custom_call" | custom-call | flops 32212254720 | bytes 10485760 | tf_op jit(solution)/shard_map/project/pallas_call | solution.py:146
  20.8 6.6 %project.5 = f32[1,80,512]{2,1,0:T(8,128)S(1)} custom-call(s32[1]{0:T(128)} %bitcast.1.refs_0_, s32[8,128]{1,0:T(8,128)} %refs_1_.7, s32[8,128]{1,0:T(8,128)} %refs_2_.7, bf16[80,65536]{1,0:T(8,128)(2,1)S(1)} %get-tuple-element.12.refs_3_), custom_call_target="tpu_custom_call" | custom-call | flops 10737418240 | bytes 10485760 | tf_op jit(solution)/shard_map/project/pallas_call | solution.py:146
  27.4 5.2 %collective-permute-start = (f32[80,512]{1,0:T(8,128)S(1)}, f32[80,512]{1,0:T(8,128)S(1)}, u32[]{:S(2)}, u32[]{:S(2)}) collective-permute-start(f32[80,512]{1,0:T(8,128)S(1)} %bitcast.9), channel_id=1, source_target_pairs={{0,240},{16,0},{32,16},{48,32},{64,48},{80,64},{96,80},{112,96},{1... | collective-permute-start | bytes 491528 | tf_op jit(solution)/shard_map/ppermute | solution.py:234
  32.6 0.5 collective-permute-start.1
  33.1 14.6 %project.7.even_ref = f32[3,80,512]{2,1,0:T(8,128)S(1)} custom-call(s32[1]{0:T(128)} %bitcast.1.refs_0_, s32[8,128]{1,0:T(8,128)} %refs_1_.7, s32[8,128]{1,0:T(8,128)} %refs_2_.7, bf16[80,65536]{1,0:T(8,128)(2,1)S(1)} %get-tuple-element.12.refs_3_), custom_call_target="tpu_custom_call" | custom-call | flops 32212254720 | bytes 10485760 | tf_op jit(solution)/shard_map/project/pallas_call | solution.py:146
  47.6 0.0 collective-permute-done.1.odd_ref
  47.7 0.1 join.1
  47.7 1.5 %collective-permute-start.2 = (f32[80,512]{1,0:T(8,128)S(1)}, f32[80,512]{1,0:T(8,128)S(1)}, u32[]{:S(2)}, u32[]{:S(2)}) collective-permute-start(f32[80,512]{1,0:T(8,128)S(1)} %get-tuple-element.14), channel_id=1, source_target_pairs={{0,192},{16,208},{32,224},{48,240},{64,0},{80,16},{96,32},{112,48}... | collective-permute-start | bytes 491528 | tf_op jit(solution)/shard_map/ppermute | solution.py:234
  49.2 0.4 collective-permute-start.3
  49.7 2.8 %collective-permute-start.4 = (f32[80,512]{1,0:T(8,128)S(1)}, f32[80,512]{1,0:T(8,128)S(1)}, u32[]{:S(2)}, u32[]{:S(2)}) collective-permute-start(f32[80,512]{1,0:T(8,128)S(1)} %get-tuple-element.16), channel_id=1, source_target_pairs={{0,64},{16,80},{32,96},{48,112},{64,128},{80,144},{96,160},{112,17... | collective-permute-start | bytes 491528 | tf_op jit(solution)/shard_map/ppermute | solution.py:234
  52.5 6.6 %project.6 = f32[1,80,512]{2,1,0:T(8,128)S(1)} custom-call(s32[1]{0:T(128)} %bitcast.1.refs_0_, s32[8,128]{1,0:T(8,128)} %refs_1_.7, s32[8,128]{1,0:T(8,128)} %refs_2_.7, bf16[80,65536]{1,0:T(8,128)(2,1)S(1)} %get-tuple-element.12.refs_3_), custom_call_target="tpu_custom_call" | custom-call | flops 10737418240 | bytes 10485760 | tf_op jit(solution)/shard_map/project/pallas_call | solution.py:146
  59.1 0.0 collective-permute-done.refs_0_
  59.1 1.5 %collective-permute-done.2.refs_2_ = f32[80,512]{1,0:T(8,128)S(1)} collective-permute-done((f32[80,512]{1,0:T(8,128)S(1)}, f32[80,512]{1,0:T(8,128)S(1)}, u32[]{:S(2)}, u32[]{:S(2)}) %collective-permute-start.2) | collective-permute-done | bytes 163872 | tf_op jit(solution)/shard_map/ppermute | solution.py:234
  60.6 4.6 %collective-permute-done.3.refs_3_ = f32[80,512]{1,0:T(8,128)S(1)} collective-permute-done((f32[80,512]{1,0:T(8,128)S(1)}, f32[80,512]{1,0:T(8,128)S(1)}, u32[]{:S(2)}, u32[]{:S(2)}) %collective-permute-start.3) | collective-permute-done | bytes 163872 | tf_op jit(solution)/shard_map/ppermute | solution.py:234
  65.2 1.3 %collective-permute-done.4.refs_4_ = f32[80,512]{1,0:T(8,128)S(1)} collective-permute-done((f32[80,512]{1,0:T(8,128)S(1)}, f32[80,512]{1,0:T(8,128)S(1)}, u32[]{:S(2)}, u32[]{:S(2)}) %collective-permute-start.4) | collective-permute-done | bytes 163872 | tf_op jit(solution)/shard_map/ppermute | solution.py:234
  66.5 0.1 merge.1
  66.6 15.4 %all_to_all.10.own_ref = f32[8,16,512]{2,1,0:T(8,128)S(1)} all-to-all(f32[8,16,512]{2,1,0:T(8,128)S(1)} %get-tuple-element.18), channel_id=1, replica_groups={{0,2,4,6,8,10,12,14},{1,3,5,7,9,11,13,15},{16,18,20,22,24,26,28,30},{17..., dimensions={0} | all-to-all | bytes 524288 | tf_op jit(solution)/shard_map/all_to_all | solution.py:268
  81.9 0.0 collective-permute-start.5
  81.9 1.5 %collective-permute-done.5.other_ref = f32[8,16,512]{2,1,0:T(8,128)S(1)} collective-permute-done((f32[8,16,512]{2,1,0:T(8,128)S(1)}, f32[8,16,512]{2,1,0:T(8,128)S(1)}, u32[]{:S(2)}, u32[]{:S(2)}) %collective-permute-start.5) | collective-permute-done | bytes 262176 | tf_op jit(solution)/shard_map/ppermute | solution.py:271
  83.5 0.6 dots.1
  84.1 16.3 %all_to_all.11.parts_ref = f32[16,24,128]{2,1,0:T(8,128)S(1)} all-to-all(f32[16,24,128]{2,1,0:T(8,128)S(1)} %bitcast.7), channel_id=1, replica_groups=mesh['feat'=16,'cand'=16] {'feat'}, dimensions={0} | all-to-all | bytes 393216 | tf_op jit(solution)/shard_map/all_to_all | solution.py:281
  100.4 0.7 score.1
Async XLA Ops:
  27.4 31.7 %collective-permute-start = (f32[80,512]{1,0:T(8,128)S(1)}, f32[80,512]{1,0:T(8,128)S(1)}, u32[]{:S(2)}, u32[]{:S(2)}) collective-permute-start(f32[80,512]{1,0:T(8,128)S(1)} %bitcast.9), channel_id=1, source_target_pairs={{0,240},{16,0},{32,16},{48,32},{64,48},{80,64},{96,80},{112,96},{1... | collective-permute-start | bytes 491528 | tf_op jit(solution)/shard_map/ppermute | solution.py:234
  32.6 15.0 %collective-permute-start.1 = (f32[3,80,512]{2,1,0:T(8,128)S(1)}, f32[3,80,512]{2,1,0:T(8,128)S(1)}, u32[]{:S(2)}, u32[]{:S(2)}) collective-permute-start(f32[3,80,512]{2,1,0:T(8,128)S(1)} %get-tuple-element.13), channel_id=1, source_target_pairs={{0,240},{16,0},{32,16},{48,32},{64,48},{80,64},{96,80},{112,96},{1... | collective-permute-start | bytes 1474568 | tf_op jit(solution)/shard_map/ppermute | solution.py:234
  47.7 12.9 %collective-permute-start.2 = (f32[80,512]{1,0:T(8,128)S(1)}, f32[80,512]{1,0:T(8,128)S(1)}, u32[]{:S(2)}, u32[]{:S(2)}) collective-permute-start(f32[80,512]{1,0:T(8,128)S(1)} %get-tuple-element.14), channel_id=1, source_target_pairs={{0,192},{16,208},{32,224},{48,240},{64,0},{80,16},{96,32},{112,48}... | collective-permute-start | bytes 491528 | tf_op jit(solution)/shard_map/ppermute | solution.py:234
  49.2 15.9 %collective-permute-start.3 = (f32[80,512]{1,0:T(8,128)S(1)}, f32[80,512]{1,0:T(8,128)S(1)}, u32[]{:S(2)}, u32[]{:S(2)}) collective-permute-start(f32[80,512]{1,0:T(8,128)S(1)} %get-tuple-element.15), channel_id=1, source_target_pairs={{0,128},{16,144},{32,160},{48,176},{64,192},{80,208},{96,224},{112... | collective-permute-start | bytes 491528 | tf_op jit(solution)/shard_map/ppermute | solution.py:234
  49.7 16.9 %collective-permute-start.4 = (f32[80,512]{1,0:T(8,128)S(1)}, f32[80,512]{1,0:T(8,128)S(1)}, u32[]{:S(2)}, u32[]{:S(2)}) collective-permute-start(f32[80,512]{1,0:T(8,128)S(1)} %get-tuple-element.16), channel_id=1, source_target_pairs={{0,64},{16,80},{32,96},{48,112},{64,128},{80,144},{96,160},{112,17... | collective-permute-start | bytes 491528 | tf_op jit(solution)/shard_map/ppermute | solution.py:234
  81.9 1.5 %collective-permute-start.5 = (f32[8,16,512]{2,1,0:T(8,128)S(1)}, f32[8,16,512]{2,1,0:T(8,128)S(1)}, u32[]{:S(2)}, u32[]{:S(2)}) collective-permute-start(f32[8,16,512]{2,1,0:T(8,128)S(1)} %all_to_all.10.own_ref), channel_id=1, source_target_pairs={{0,1},{1,0},{2,3},{3,2},{4,5},{5,4},{6,7},{7,6},{8,9},{9,8},{10,11... | collective-permute-start | bytes 786440 | tf_op jit(solution)/shard_map/ppermute | solution.py:271

commit v5 on v4

--- a/solution.py
+++ b/solution.py
@@ -82,10 +82,12 @@
 
             for copy in copies(block):
                 copy.wait()
-            wide = cand_ref[:, at].astype(jnp.float32)
-            square = 0.999 * moment_ref[:, at] + (0.001 * wide) * wide
-            den = square * lax.rsqrt(square) + 1e-08
-            rows_ref[: cand_ref.shape[0], at] = (wide * lax.rsqrt(den * den)).astype(jnp.bfloat16)
+            moment = jnp.broadcast_to(0.999 * moment_ref[:, at], (16, PB))
+            for row in range(0, cand_ref.shape[0], 16):
+                wide = cand_ref[row : row + 16, at].astype(jnp.float32)
+                square = moment + (0.001 * wide) * wide
+                den = square * lax.rsqrt(square) + 1e-08
+                rows_ref[row : row + 16, at] = (wide * lax.rsqrt(den * den)).astype(jnp.bfloat16)
         mixed = []
         for n in range(count):
             mixed.append(column ^ fold(table_ref[0, n, block]))

time: 103 us -> 103 us (level)
  no operation moved by 1% of the time
where the time goes in v5:
time: 103 us; the launch traced here: 101 us
  Pallas kernels  49.9 us (48%)
  blocking collectives  31.6 us (31%)
  starting transfers between devices  10.5 us (10%)
  waiting for transfers between devices  8.96 us (9%)
    pallas_call x4, Pallas kernels, projected(): pl.pallas_call(lambda *refs: project(slots, adam, devices, *refs), out_sh...  48.5 us
    all_to_all x1, blocking collectives, body(): parts = lax.all_to_all(packed, 'feat', 0, 0, tiled=True)  16.3 us
    all_to_all x1, blocking collectives, body(): lax.all_to_all(val_part, 'cand', 0, 0, tiled=True, axis_index_groups=same...  15.3 us
    ppermute x5, starting transfers between devices, back(): lax.ppermute(part, 'feat', [(j, (j - steps) % devices) for j in range(dev...  10.5 us
    ppermute x5, waiting for transfers between devices, back(): lax.ppermute(part, 'feat', [(j, (j - steps) % devices) for j in range(dev...  7.43 us
  transfers between devices with their start and end apart: 6, of which 4 were waited for; matrix products, arithmetic and copies ran while one was open for 0% of the time, Pallas kernels for 21%

profile of v5, /device:TPU:0, one launch (start us, length us, event | category | flops | bytes accessed | tf_op | source)
XLA Modules:
  0.0 101.0 jit_solution(13818020148046520417)
XLA Ops:
  0.0 20.8 %project.4 = (f32[3,80,512]{2,1,0:T(8,128)S(1)}, bf16[80,65536]{1,0:T(8,128)(2,1)S(1)}) custom-call(s32[1]{0:T(128)} %bitcast.1.refs_0_, s32[8,128]{1,0:T(8,128)} %refs_1_.7, s32[8,128]{1,0:T(8,128)} %refs_2_.7, bf16[64,65536]{1,0:T(8,128)(2,1)} %refs_3_.1, bf16[16,65536]{1,0:T(8,128)(2,1)} %refs_4_.1, f32[1,65536]{1,0:T(1,128)} %bitcast.10), custom_call_target="tpu_custom_call" | custom-call | flops 32212254720 | bytes 10485760 | tf_op jit(solution)/shard_map/project/pallas_call | solution.py:148
  20.8 6.6 %project.5 = f32[1,80,512]{2,1,0:T(8,128)S(1)} custom-call(s32[1]{0:T(128)} %bitcast.1.refs_0_, s32[8,128]{1,0:T(8,128)} %refs_1_.7, s32[8,128]{1,0:T(8,128)} %refs_2_.7, bf16[80,65536]{1,0:T(8,128)(2,1)S(1)} %get-tuple-element.12.refs_3_), custom_call_target="tpu_custom_call" | custom-call | flops 10737418240 | bytes 10485760 | tf_op jit(solution)/shard_map/project/pallas_call | solution.py:148
  27.4 5.2 %collective-permute-start = (f32[80,512]{1,0:T(8,128)S(1)}, f32[80,512]{1,0:T(8,128)S(1)}, u32[]{:S(2)}, u32[]{:S(2)}) collective-permute-start(f32[80,512]{1,0:T(8,128)S(1)} %bitcast.9), channel_id=1, source_target_pairs={{0,240},{16,0},{32,16},{48,32},{64,48},{80,64},{96,80},{112,96},{1... | collective-permute-start | bytes 491528 | tf_op jit(solution)/shard_map/ppermute | solution.py:236
  32.6 0.5 collective-permute-start.1
  33.1 14.6 %project.7.even_ref = f32[3,80,512]{2,1,0:T(8,128)S(1)} custom-call(s32[1]{0:T(128)} %bitcast.1.refs_0_, s32[8,128]{1,0:T(8,128)} %refs_1_.7, s32[8,128]{1,0:T(8,128)} %refs_2_.7, bf16[80,65536]{1,0:T(8,128)(2,1)S(1)} %get-tuple-element.12.refs_3_), custom_call_target="tpu_custom_call" | custom-call | flops 32212254720 | bytes 10485760 | tf_op jit(solution)/shard_map/project/pallas_call | solution.py:148
  47.6 0.0 collective-permute-done.1.odd_ref
  47.6 0.1 join.1
  47.7 1.5 %collective-permute-start.2 = (f32[80,512]{1,0:T(8,128)S(1)}, f32[80,512]{1,0:T(8,128)S(1)}, u32[]{:S(2)}, u32[]{:S(2)}) collective-permute-start(f32[80,512]{1,0:T(8,128)S(1)} %get-tuple-element.14), channel_id=1, source_target_pairs={{0,192},{16,208},{32,224},{48,240},{64,0},{80,16},{96,32},{112,48}... | collective-permute-start | bytes 491528 | tf_op jit(solution)/shard_map/ppermute | solution.py:236
  49.2 0.4 collective-permute-start.3
  49.6 2.8 %collective-permute-start.4 = (f32[80,512]{1,0:T(8,128)S(1)}, f32[80,512]{1,0:T(8,128)S(1)}, u32[]{:S(2)}, u32[]{:S(2)}) collective-permute-start(f32[80,512]{1,0:T(8,128)S(1)} %get-tuple-element.16), channel_id=1, source_target_pairs={{0,64},{16,80},{32,96},{48,112},{64,128},{80,144},{96,160},{112,17... | collective-permute-start | bytes 491528 | tf_op jit(solution)/shard_map/ppermute | solution.py:236
  52.5 6.6 %project.6 = f32[1,80,512]{2,1,0:T(8,128)S(1)} custom-call(s32[1]{0:T(128)} %bitcast.1.refs_0_, s32[8,128]{1,0:T(8,128)} %refs_1_.7, s32[8,128]{1,0:T(8,128)} %refs_2_.7, bf16[80,65536]{1,0:T(8,128)(2,1)S(1)} %get-tuple-element.12.refs_3_), custom_call_target="tpu_custom_call" | custom-call | flops 10737418240 | bytes 10485760 | tf_op jit(solution)/shard_map/project/pallas_call | solution.py:148
  59.0 0.0 collective-permute-done.refs_0_
  59.1 1.5 %collective-permute-done.2.refs_2_ = f32[80,512]{1,0:T(8,128)S(1)} collective-permute-done((f32[80,512]{1,0:T(8,128)S(1)}, f32[80,512]{1,0:T(8,128)S(1)}, u32[]{:S(2)}, u32[]{:S(2)}) %collective-permute-start.2) | collective-permute-done | bytes 163872 | tf_op jit(solution)/shard_map/ppermute | solution.py:236
  60.6 4.6 %collective-permute-done.3.refs_3_ = f32[80,512]{1,0:T(8,128)S(1)} collective-permute-done((f32[80,512]{1,0:T(8,128)S(1)}, f32[80,512]{1,0:T(8,128)S(1)}, u32[]{:S(2)}, u32[]{:S(2)}) %collective-permute-start.3) | collective-permute-done | bytes 163872 | tf_op jit(solution)/shard_map/ppermute | solution.py:236
  65.1 1.3 %collective-permute-done.4.refs_4_ = f32[80,512]{1,0:T(8,128)S(1)} collective-permute-done((f32[80,512]{1,0:T(8,128)S(1)}, f32[80,512]{1,0:T(8,128)S(1)}, u32[]{:S(2)}, u32[]{:S(2)}) %collective-permute-start.4) | collective-permute-done | bytes 163872 | tf_op jit(solution)/shard_map/ppermute | solution.py:236
  66.5 0.1 merge.1
  66.5 15.3 %all_to_all.10.own_ref = f32[8,16,512]{2,1,0:T(8,128)S(1)} all-to-all(f32[8,16,512]{2,1,0:T(8,128)S(1)} %get-tuple-element.18), channel_id=1, replica_groups={{0,2,4,6,8,10,12,14},{1,3,5,7,9,11,13,15},{16,18,20,22,24,26,28,30},{17..., dimensions={0} | all-to-all | bytes 524288 | tf_op jit(solution)/shard_map/all_to_all | solution.py:270
  81.9 0.0 collective-permute-start.5
  81.9 1.5 %collective-permute-done.5.other_ref = f32[8,16,512]{2,1,0:T(8,128)S(1)} collective-permute-done((f32[8,16,512]{2,1,0:T(8,128)S(1)}, f32[8,16,512]{2,1,0:T(8,128)S(1)}, u32[]{:S(2)}, u32[]{:S(2)}) %collective-permute-start.5) | collective-permute-done | bytes 262176 | tf_op jit(solution)/shard_map/ppermute | solution.py:273
  83.4 0.6 dots.1
  84.1 16.3 %all_to_all.11.parts_ref = f32[16,24,128]{2,1,0:T(8,128)S(1)} all-to-all(f32[16,24,128]{2,1,0:T(8,128)S(1)} %bitcast.7), channel_id=1, replica_groups=mesh['feat'=16,'cand'=16] {'feat'}, dimensions={0} | all-to-all | bytes 393216 | tf_op jit(solution)/shard_map/all_to_all | solution.py:283
  100.3 0.7 score.1
Async XLA Ops:
  27.4 31.7 %collective-permute-start = (f32[80,512]{1,0:T(8,128)S(1)}, f32[80,512]{1,0:T(8,128)S(1)}, u32[]{:S(2)}, u32[]{:S(2)}) collective-permute-start(f32[80,512]{1,0:T(8,128)S(1)} %bitcast.9), channel_id=1, source_target_pairs={{0,240},{16,0},{32,16},{48,32},{64,48},{80,64},{96,80},{112,96},{1... | collective-permute-start | bytes 491528 | tf_op jit(solution)/shard_map/ppermute | solution.py:236
  32.6 15.0 %collective-permute-start.1 = (f32[3,80,512]{2,1,0:T(8,128)S(1)}, f32[3,80,512]{2,1,0:T(8,128)S(1)}, u32[]{:S(2)}, u32[]{:S(2)}) collective-permute-start(f32[3,80,512]{2,1,0:T(8,128)S(1)} %get-tuple-element.13), channel_id=1, source_target_pairs={{0,240},{16,0},{32,16},{48,32},{64,48},{80,64},{96,80},{112,96},{1... | collective-permute-start | bytes 1474568 | tf_op jit(solution)/shard_map/ppermute | solution.py:236
  47.7 12.9 %collective-permute-start.2 = (f32[80,512]{1,0:T(8,128)S(1)}, f32[80,512]{1,0:T(8,128)S(1)}, u32[]{:S(2)}, u32[]{:S(2)}) collective-permute-start(f32[80,512]{1,0:T(8,128)S(1)} %get-tuple-element.14), channel_id=1, source_target_pairs={{0,192},{16,208},{32,224},{48,240},{64,0},{80,16},{96,32},{112,48}... | collective-permute-start | bytes 491528 | tf_op jit(solution)/shard_map/ppermute | solution.py:236
  49.2 15.9 %collective-permute-start.3 = (f32[80,512]{1,0:T(8,128)S(1)}, f32[80,512]{1,0:T(8,128)S(1)}, u32[]{:S(2)}, u32[]{:S(2)}) collective-permute-start(f32[80,512]{1,0:T(8,128)S(1)} %get-tuple-element.15), channel_id=1, source_target_pairs={{0,128},{16,144},{32,160},{48,176},{64,192},{80,208},{96,224},{112... | collective-permute-start | bytes 491528 | tf_op jit(solution)/shard_map/ppermute | solution.py:236
  49.6 16.8 %collective-permute-start.4 = (f32[80,512]{1,0:T(8,128)S(1)}, f32[80,512]{1,0:T(8,128)S(1)}, u32[]{:S(2)}, u32[]{:S(2)}) collective-permute-start(f32[80,512]{1,0:T(8,128)S(1)} %get-tuple-element.16), channel_id=1, source_target_pairs={{0,64},{16,80},{32,96},{48,112},{64,128},{80,144},{96,160},{112,17... | collective-permute-start | bytes 491528 | tf_op jit(solution)/shard_map/ppermute | solution.py:236
  81.9 1.5 %collective-permute-start.5 = (f32[8,16,512]{2,1,0:T(8,128)S(1)}, f32[8,16,512]{2,1,0:T(8,128)S(1)}, u32[]{:S(2)}, u32[]{:S(2)}) collective-permute-start(f32[8,16,512]{2,1,0:T(8,128)S(1)} %all_to_all.10.own_ref), channel_id=1, source_target_pairs={{0,1},{1,0},{2,3},{3,2},{4,5},{5,4},{6,7},{7,6},{8,9},{9,8},{10,11... | collective-permute-start | bytes 786440 | tf_op jit(solution)/shard_map/ppermute | solution.py:273
